TPU v7x, 512 devices: a whole 4x8x8 slice. The times are simulated.
512 devices in a mesh: gx: 32 (over y, x), gy: 16 (over z, core).
Axes of the slice: x: 4, y: 8, z: 8, core: 2. Of those that a mesh axis runs over, the one named last changes fastest.
Arguments:
- solution: float32 [32, 16, 8, 8, 8, 128], P('gx', 'gy'), as said below
- residual: float32 [32, 16, 8, 8, 8, 128], P('gx', 'gy'), as said below
- grain_counts: int32 [32, 16, 128], P('gx', 'gy'), may hold values from 0 to 16
Outputs:
- solution_out: float32 [32, 16, 8, 8, 8, 128], P('gx', 'gy')
- residual_out: float32 [32, 16, 8, 8, 8, 128], P('gx', 'gy')
- direction_out: float32 [32, 16, 8, 8, 8, 128], P('gx', 'gy')
- step_sizes: float32 [2], replicated
Inputs may be any that keep to these rules, and one draw needn't show every extreme that they name: `solution`: every node shared by neighbouring elements holds the same value in all of its copies. `residual`: every node shared by neighbouring elements holds the same value in all of its copies.
All inputs are finite; a program needn't handle non-finite values.
Results may differ from a plain program's by a relative error of at most 0.003.
Values sent between devices are 32-bit elements; how exact they have to be, the bound alone decides.
A program may use at most 64 MiB of HBM per device.

v0:
```python
import math

import jax
import jax.numpy as jnp
import numpy as np
from jax import lax
from jax.sharding import PartitionSpec as P

NODES = 8
MOST_GRAINS = 16
ITERS = 2


shift_mass = 0.1
mean_porosity = 0.7
exact_mode = lax.Precision.HIGHEST


def padded_2(block, sides, width):
    for axis, dim in sides:
        count = lax.axis_size(axis)
        forward = [(i, i + 1) for i in range(count - 1)]
        backward = [(target, source) for source, target in forward]
        low = lax.ppermute(
            lax.slice_in_dim(block, block.shape[dim] - width, None, axis=dim), axis, forward
        )
        high = lax.ppermute(lax.slice_in_dim(block, 0, width, axis=dim), axis, backward)
        block = jnp.concatenate([low, block, high], axis=dim)
    return block


def legendre_columns(node_set, degree):
    table = [node_set * 0.0 + 1.0, node_set]
    for order in range(2, degree + 1):
        table.append(
            ((2 * order - 1) * node_set * table[order - 1] - (order - 1) * table[order - 2]) / order
        )
    return table


def gll_tables():
    degree = NODES - 1
    node_set = np.cos(math.pi * np.arange(degree + 1) / degree)
    for sweep in range(100):
        table = legendre_columns(node_set, degree)
        node_set = node_set - (node_set * table[degree] - table[degree - 1]) / (
            (degree + 1) * table[degree]
        )
    node_set = node_set[::-1].copy()
    values = legendre_columns(node_set, degree)[degree]
    weights = 2.0 / (degree * (degree + 1) * values**2)
    derivative = np.zeros((NODES, NODES))
    for row_index in range(NODES):
        for column_index in range(NODES):
            if row_index != column_index:
                derivative[row_index, column_index] = values[row_index] / (
                    values[column_index] * (node_set[row_index] - node_set[column_index])
                )
    derivative[0, 0] = -degree * (degree + 1) / 4.0
    derivative[NODES - 1, NODES - 1] = degree * (degree + 1) / 4.0
    return (weights, derivative)


def jacobi_eigen(matrix):
    size_now = matrix.shape[0]
    current = matrix.copy()
    vectors = np.eye(size_now)
    for sweep in range(12):
        for first in range(size_now - 1):
            for second in range(first + 1, size_now):
                off_value = current[first, second]
                safe_value = np.where(off_value == 0.0, 1e-300, off_value)
                theta = (current[second, second] - current[first, first]) / (2.0 * safe_value)
                sign_value = np.where(theta >= 0.0, 1.0, -1.0)
                tangent = sign_value / (np.abs(theta) + np.sqrt(theta * theta + 1.0))
                cosine = 1.0 / np.sqrt(tangent * tangent + 1.0)
                sine = tangent * cosine
                rotation = np.eye(size_now)
                rotation[first, first] = cosine
                rotation[second, second] = cosine
                rotation[first, second] = sine
                rotation[second, first] = -sine
                current = rotation.T @ current @ rotation
                vectors = vectors @ rotation
    eigen_values = np.array([current[index, index] for index in range(size_now)])
    return (eigen_values, vectors)


def schwarz_tables():
    weights, derivative = gll_tables()
    stiffness = derivative.T @ (weights[:, None] * derivative)
    total_nodes = 3 * (NODES - 1) + 1
    three_stiffness = np.zeros((total_nodes, total_nodes))
    three_mass = np.zeros(total_nodes)
    for element in range(3):
        start_node = element * (NODES - 1)
        three_stiffness[
            start_node : start_node + NODES, start_node : start_node + NODES
        ] += stiffness
        three_mass[start_node : start_node + NODES] += weights
    chosen = np.array([NODES - 2] + list(range(NODES - 1, 2 * NODES - 1)) + [2 * NODES - 1])
    local_stiffness = three_stiffness[chosen][:, chosen]
    local_mass = three_mass[chosen]
    scaling = 1.0 / np.sqrt(local_mass)
    symmetric = scaling[:, None] * local_stiffness * scaling[None, :]
    symmetric = 0.5 * (symmetric + symmetric.T)
    eigen_values, eigen_vectors = jacobi_eigen(symmetric)
    return (scaling[:, None] * eigen_vectors, eigen_values)


def cosine_basis(column_count):
    position = jnp.arange(column_count, dtype=jnp.float32)
    phase_table = math.pi * (position[:, None] + 0.5) * position[None, :] / column_count
    norm_factor = jnp.where(
        position == 0, math.sqrt(1.0 / column_count), math.sqrt(2.0 / column_count)
    )
    eigen_basis = jnp.cos(phase_table) * norm_factor[None, :]
    eigen_values = 2.0 - 2.0 * jnp.cos(math.pi * position / column_count)
    return (eigen_basis, eigen_values)


def coarse_solve(coarse_source, column_length):
    basis_first, eigen_first = cosine_basis(coarse_source.shape[0])
    basis_second, eigen_second = cosine_basis(coarse_source.shape[1])
    spectrum = jnp.einsum(
        "pa,pq,qb->ab", basis_first, coarse_source, basis_second, precision=exact_mode
    )
    divisor = (
        2.0 * mean_porosity * column_length * (eigen_first[:, None] + eigen_second[None, :])
        + 8.0 * shift_mass * column_length
    )
    return jnp.einsum(
        "pa,ab,qb->pq", basis_first, spectrum / divisor, basis_second, precision=exact_mode
    )


def share_weights(column_count, points):
    column = jnp.arange(column_count)
    identity = (column[:, None] == column[None, :]).astype(jnp.float32)
    left_side = (column[None, :] == column[:, None] - 1).astype(jnp.float32)
    right_side = (column[None, :] == column[:, None] + 1).astype(jnp.float32)
    has_left = (column > 0).astype(jnp.float32)
    has_right = (column < column_count - 1).astype(jnp.float32)
    lowest = identity * (1.0 - 0.5 * has_left[:, None]) + 0.5 * left_side
    highest = identity * (1.0 - 0.5 * has_right[:, None]) + 0.5 * right_side
    table = jnp.broadcast_to(identity[:, None, :], (column_count, points, column_count))
    return table.at[:, 0, :].set(lowest).at[:, points - 1, :].set(highest)


def multiplicity_inverse(column_count, points):
    column = jnp.arange(column_count)[:, None]
    node_index = jnp.arange(points)[None, :]
    shared = (node_index == 0) & (column > 0) | (node_index == points - 1) & (
        column < column_count - 1
    )
    return 1.0 / (1.0 + shared.astype(jnp.float32))


def shift_elements(layers, element_axis, toward):
    extent = layers.shape[element_axis]
    widths = [(0, 0)] * layers.ndim
    if toward > 0:
        retained = lax.slice_in_dim(layers, 0, extent - 1, axis=element_axis)
        widths[element_axis] = (1, 0)
    else:
        retained = lax.slice_in_dim(layers, 1, extent, axis=element_axis)
        widths[element_axis] = (0, 1)
    return jnp.pad(retained, widths)


def extend(nodal_field, node_axis, element_axis):
    points = nodal_field.shape[node_axis]
    lower_layer = shift_elements(
        lax.slice_in_dim(nodal_field, points - 2, points - 1, axis=node_axis), element_axis, 1
    )
    upper_layer = shift_elements(
        lax.slice_in_dim(nodal_field, 1, 2, axis=node_axis), element_axis, -1
    )
    return jnp.concatenate([lower_layer, nodal_field, upper_layer], axis=node_axis)


def spread(extended, node_axis, element_axis):
    points = extended.shape[node_axis] - 2
    own_part = lax.slice_in_dim(extended, 1, points + 1, axis=node_axis)
    lower_layer = shift_elements(
        lax.slice_in_dim(extended, points, points + 2, axis=node_axis), element_axis, 1
    )
    upper_layer = shift_elements(lax.slice_in_dim(extended, 0, 2, axis=node_axis), element_axis, -1)
    lower_widths = [(0, 0)] * extended.ndim
    lower_widths[node_axis] = (0, points - 2)
    upper_widths = [(0, 0)] * extended.ndim
    upper_widths[node_axis] = (points - 2, 0)
    return own_part + jnp.pad(lower_layer, lower_widths) + jnp.pad(upper_layer, upper_widths)


def schwarz_solve(extended, eigen_basis, eigen_values):
    first_pass = jnp.einsum("ia,...ijke->...ajke", eigen_basis, extended, precision=exact_mode)
    second_pass = jnp.einsum("jb,...ajke->...abke", eigen_basis, first_pass, precision=exact_mode)
    third_pass = jnp.einsum("kc,...abke->...abce", eigen_basis, second_pass, precision=exact_mode)
    divisor = (
        mean_porosity
        * (eigen_values[:, None, None] + eigen_values[None, :, None] + eigen_values[None, None, :])
        + shift_mass
    )
    scaled = third_pass / divisor[..., None]
    back_first = jnp.einsum("ia,...abce->...ibce", eigen_basis, scaled, precision=exact_mode)
    back_second = jnp.einsum("jb,...ibce->...ijce", eigen_basis, back_first, precision=exact_mode)
    return jnp.einsum("kc,...ijce->...ijke", eigen_basis, back_second, precision=exact_mode)


def apply_local(nodal_field, coupling, derivative, weights_cube):
    grad_first = jnp.einsum("ai,...ijke->...ajke", derivative, nodal_field, precision=exact_mode)
    flux_first = jnp.einsum(
        "ai,...ajke->...ijke", derivative, coupling * grad_first, precision=exact_mode
    )
    grad_second = jnp.einsum("bj,...ijke->...ibke", derivative, nodal_field, precision=exact_mode)
    flux_second = jnp.einsum(
        "bj,...ibke->...ijke", derivative, coupling * grad_second, precision=exact_mode
    )
    grad_third = jnp.einsum("ck,...ijke->...ijce", derivative, nodal_field, precision=exact_mode)
    flux_third = jnp.einsum(
        "ck,...ijce->...ijke", derivative, coupling * grad_third, precision=exact_mode
    )
    return (
        flux_first + flux_second + flux_third + shift_mass * weights_cube[..., None] * nodal_field
    )


def assemble_z(nodal_field):
    points = nodal_field.shape[-2]
    shared = nodal_field[..., points - 1, :-1] + nodal_field[..., 0, 1:]
    return nodal_field.at[..., points - 1, :-1].set(shared).at[..., 0, 1:].set(shared)


def collect(padded, axis_number, halo_width, skipped):
    extent = padded.shape[axis_number]
    points = extent - 2 * halo_width - 2 * skipped
    core_part = lax.slice_in_dim(
        padded, halo_width + skipped, halo_width + skipped + points, axis=axis_number
    )
    lower_layer = lax.slice_in_dim(padded, 0, halo_width, axis=axis_number)
    upper_layer = lax.slice_in_dim(padded, extent - halo_width, extent, axis=axis_number)
    lower_widths = [(0, 0)] * padded.ndim
    lower_widths[axis_number] = (0, points - halo_width)
    upper_widths = [(0, 0)] * padded.ndim
    upper_widths[axis_number] = (points - halo_width, 0)
    return core_part + jnp.pad(lower_layer, lower_widths) + jnp.pad(upper_layer, upper_widths)


def pick_frame(framed, axis_number):
    extent = framed.shape[axis_number]
    return jnp.concatenate(
        [
            lax.slice_in_dim(framed, 0, 1, axis=axis_number),
            lax.slice_in_dim(framed, 2, extent - 2, axis=axis_number),
            lax.slice_in_dim(framed, extent - 1, extent, axis=axis_number),
        ],
        axis=axis_number,
    )


def shards(solution, residual, grain_counts):
    weights_np, derivative_np = gll_tables()
    weights = jnp.asarray(weights_np, dtype=jnp.float32)
    derivative = jnp.asarray(derivative_np, dtype=jnp.float32)
    weights_cube = weights[:, None, None] * weights[None, :, None] * weights[None, None, :]
    basis_np, eigen_np = schwarz_tables()
    eigen_basis = jnp.asarray(basis_np, dtype=jnp.float32)
    eigen_values = jnp.asarray(eigen_np, dtype=jnp.float32)
    shard_shape = solution.shape
    points = shard_shape[2]
    column_length = shard_shape[5]
    solution = solution.reshape(shard_shape[2:])
    residual = residual.reshape(shard_shape[2:])
    porosity = 1.0 - 0.6 * grain_counts.reshape(column_length).astype(jnp.float32) / MOST_GRAINS
    coupling = weights_cube[..., None] * porosity[None, None, None, :]
    count_first = lax.axis_size("gx")
    count_second = lax.axis_size("gy")
    index_first = lax.axis_index("gx")
    index_second = lax.axis_index("gy")
    inverse_first = lax.dynamic_index_in_dim(
        multiplicity_inverse(count_first, points), index_first, 0, keepdims=False
    )
    inverse_second = lax.dynamic_index_in_dim(
        multiplicity_inverse(count_second, points), index_second, 0, keepdims=False
    )
    inverse_third = multiplicity_inverse(column_length, points).T
    inverse_all = (
        inverse_first[:, None, None, None]
        * inverse_second[None, :, None, None]
        * inverse_third[None, None, :, :]
    )
    share_first = lax.dynamic_index_in_dim(
        share_weights(count_first, points), index_first, 0, keepdims=False
    )
    share_second = lax.dynamic_index_in_dim(
        share_weights(count_second, points), index_second, 0, keepdims=False
    )
    residual_frame = residual
    coarse_source = jnp.zeros((count_first, count_second), jnp.float32)
    direction = residual
    previous_inner = jnp.float32(1.0)
    step_list = []
    for step_index in range(ITERS):
        residual_frame = padded_2(residual, (("gx", 0), ("gy", 1)), 2)
        columns = jnp.sum(inverse_all * residual, axis=(2, 3))
        coarse_source = lax.psum(
            jnp.einsum("ij,ia,jb->ab", columns, share_first, share_second, precision=exact_mode),
            ("gx", "gy"),
        )
        extended = extend(pick_frame(pick_frame(residual_frame, 0), 1), 2, 3)
        local_solution = schwarz_solve(extended, eigen_basis, eigen_values)
        partial_value = spread(local_solution, 2, 3)
        padded = padded_2(partial_value, (("gx", 0), ("gy", 1)), 2)
        schwarz_part = collect(collect(padded, 0, 2, 1), 1, 2, 1)
        coarse_field = coarse_solve(coarse_source, column_length)
        lifted = jnp.einsum(
            "ia,ab,jb->ij", share_first, coarse_field, share_second, precision=exact_mode
        )
        preconditioned = schwarz_part + lifted[:, :, None, None]
        precond_inner = lax.psum(jnp.sum(inverse_all * residual * preconditioned), ("gx", "gy"))
        if step_index == 0:
            direction = preconditioned
        else:
            direction = preconditioned + precond_inner / previous_inner * direction
        image_local = assemble_z(apply_local(direction, coupling, derivative, weights_cube))
        padded = padded_2(image_local, (("gx", 0), ("gy", 1)), 1)
        image = collect(collect(padded, 0, 1, 0), 1, 1, 0)
        local_curvature = jnp.sum(inverse_all * direction * image)
        curvature = lax.psum(local_curvature, ("gx", "gy"))
        step_size = precond_inner / curvature
        solution = solution + step_size * direction
        residual = residual - step_size * image
        previous_inner = precond_inner
        step_list.append(step_size)
    return (
        solution.reshape(shard_shape),
        residual.reshape(shard_shape),
        direction.reshape(shard_shape),
        jnp.stack(step_list),
    )


def solution(mesh):
    return jax.shard_map(
        shards,
        mesh=mesh,
        in_specs=(
            P("gx", "gy", None, None, None, None),
            P("gx", "gy", None, None, None, None),
            P("gx", "gy", None),
        ),
        out_specs=(
            P("gx", "gy", None, None, None, None),
            P("gx", "gy", None, None, None, None),
            P("gx", "gy", None, None, None, None),
            P(),
        ),
        check_vma=False,
    )
```

profile of v0, /device:TPU:1, one launch (start us, length us, event | category | flops | bytes accessed | tf_op | source)
XLA Modules:
  0.0 663.8 jit_solution(1539824277509560193)
XLA Ops:
  1.8 4.1 collective-permute-start
  10.6 106.7 %psum.42 = f32[32,16]{0,1:T(8,128)S(1)} all-reduce(f32[32,16]{0,1:T(8,128)S(1)} %fusion.148), channel_id=1, replica_groups=mesh['gx'=32,'gy'=16] {'gx','gy'}, use_global_device_ids=true, to_apply=%region_1.2 | all-reduce | flops 512 | bytes 4096 | tf_op jit(solution)/shard_map/psum | solution.py:307
  118.5 3.3 collective-permute-start.2
  123.9 4.2 collective-permute-done.3
  136.1 3.7 collective-permute-start.4
  141.3 3.7 collective-permute-done.5
  145.1 3.2 collective-permute-start.6
  151.0 3.6 collective-permute-done.7
  164.9 3.8 collective-permute-done.9
  173.7 3.6 collective-permute-done.11
  178.5 104.2 %all-reduce.20 = (f32[]{:T(128)}, f32[]{:T(128)}) all-reduce(f32[]{:T(128)} %get-tuple-element.117, f32[]{:T(128)} %get-tuple-element.116), channel_id=1, replica_groups=mesh['gx'=32,'gy'=16] {'gx','gy'}, use_global_device_ids=true, to_apply=%region_3.4 | all-reduce | flops 2 | bytes 16 | tf_op jit(solution)/shard_map/psum | solution.py:321
  284.7 94.8 %psum.45 = f32[32,16]{0,1:T(8,128)S(1)} all-reduce(f32[32,16]{0,1:T(8,128)S(1)} %fusion.144), channel_id=1, replica_groups=mesh['gx'=32,'gy'=16] {'gx','gy'}, use_global_device_ids=true, to_apply=%region_7.8 | all-reduce | flops 512 | bytes 4096 | tf_op jit(solution)/shard_map/psum | solution.py:307
  380.1 3.7 collective-permute-start.12
  385.4 3.4 collective-permute-done.13
  388.9 3.9 collective-permute-start.14
  395.2 3.9 collective-permute-done.15
  409.6 3.7 collective-permute-done.17
  413.4 3.2 collective-permute-start.18
  418.7 4.2 collective-permute-done.19
  424.2 105.3 %psum.46 = f32[]{:T(128)} all-reduce(f32[]{:T(128)} %multiply_reduce_fusion), channel_id=1, replica_groups=mesh['gx'=32,'gy'=16] {'gx','gy'}, use_global_device_ids=true, to_apply=%region_9.10 | all-reduce | flops 1 | bytes 8 | tf_op jit(solution)/shard_map/psum | solution.py:321
  540.1 3.3 collective-permute-done.21
  543.4 3.5 collective-permute-start.22
  548.9 3.6 collective-permute-done.23
  554.4 104.8 %psum.47 = f32[]{:T(128)} all-reduce(f32[]{:T(128)} %fusion.75), channel_id=1, replica_groups=mesh['gx'=32,'gy'=16] {'gx','gy'}, use_global_device_ids=true, to_apply=%region_11.12 | all-reduce | flops 1 | bytes 8 | tf_op jit(solution)/shard_map/psum | solution.py:330
  (192 shorter events, 72.5 us)
Async XLA Ops:
  1.8 116.7 %collective-permute-start = (f32[2,8,8,128]{3,0,2,1:T(2,128)S(1)}, f32[2,8,8,128]{3,0,2,1:T(2,128)S(1)}, u32[]{:S(2)}, u32[]{:S(2)}) collective-permute-start(f32[2,8,8,128]{3,0,2,1:T(2,128)S(1)} %get-tuple-element.156), channel_id=1, source_target_pairs={{0,16},{16,32},{32,48},{48,64},{64,80},{80,96},{96,112},{112,128},... | collective-permute-start | bytes 196616 | tf_op jit(solution)/shard_map/ppermute | solution.py:24
  5.9 112.6 %collective-permute-start.1 = (f32[2,8,8,128]{3,0,2,1:T(2,128)S(1)}, f32[2,8,8,128]{3,0,2,1:T(2,128)S(1)}, u32[]{:S(2)}, u32[]{:S(2)}) collective-permute-start(f32[2,8,8,128]{3,0,2,1:T(2,128)S(1)} %get-tuple-element.157), channel_id=1, source_target_pairs={{16,0},{32,16},{48,32},{64,48},{80,64},{96,80},{112,96},{128,112},... | collective-permute-start | bytes 196616 | tf_op jit(solution)/shard_map/ppermute | solution.py:27
  118.5 5.3 collective-permute-start.2
  121.8 6.3 collective-permute-start.3
  136.1 5.2 collective-permute-start.4
  139.8 5.2 collective-permute-start.5
  145.1 5.9 collective-permute-start.6
  148.3 6.3 collective-permute-start.7
  161.9 3.0 collective-permute-start.8
  163.6 5.1 collective-permute-start.9
  168.7 4.9 collective-permute-start.10
  171.8 5.6 collective-permute-start.11
  380.1 5.3 collective-permute-start.12
  383.8 5.0 collective-permute-start.13
  388.9 6.3 collective-permute-start.14
  392.8 6.3 collective-permute-start.15
  406.5 3.1 collective-permute-start.16
  408.2 5.2 collective-permute-start.17
  413.4 5.3 collective-permute-start.18
  416.6 6.3 collective-permute-start.19
  537.1 2.9 collective-permute-start.20
  538.8 4.7 collective-permute-start.21
  543.4 5.4 collective-permute-start.22
  547.0 5.6 collective-permute-start.23
  (9 other events, 26.0 us)
where the time goes:
time: 665 us; the launch traced here: 664 us
  blocking collectives  516 us (78%)
  starting transfers between devices  56.1 us (8%)
  waiting for transfers between devices  41.3 us (6%)
  matrix products  21.7 us (3%)
  local copies, waits for them, and re-layouts  14.2 us (2%)
  other arithmetic  8.98 us (1%)
    psum x2, blocking collectives, shards(): lax.psum(jnp.sum(inverse_all * residual * preconditioned), ('gx', 'gy'))  209 us
    psum x2, blocking collectives, shards(): lax.psum(jnp.einsum('ij,ia,jb->ab', columns, share_first, share_second, p...  201 us
    psum x1, blocking collectives, shards(): curvature = lax.psum(local_curvature, ('gx', 'gy'))  105 us
    ppermute x12, waiting for transfers between devices, padded_2(): lax.ppermute(lax.slice_in_dim(block, 0, width, axis=dim), axis, backward)  41.2 us
    ppermute x12, starting transfers between devices, padded_2(): lax.ppermute(lax.slice_in_dim(block, block.shape[dim] - width, None, axis...  36.4 us
    ppermute x12, starting transfers between devices, padded_2(): lax.ppermute(lax.slice_in_dim(block, 0, width, axis=dim), axis, backward)  19.7 us
  transfers between devices with their start and end apart: 24, of which 11 were waited for; matrix products, arithmetic and copies ran while one was open for 1% of the time, Pallas kernels for 0%

commit v1 on v0

v1 whole, which is shorter than its diff:
```python
import functools
import math

import jax
import jax.numpy as jnp
import ml_dtypes
import numpy as np
from jax import lax
from jax.experimental import pallas as pl
from jax.experimental.pallas import tpu as pltpu
from jax.sharding import PartitionSpec as P

N = 8
MOST_GRAINS = 16
shift_mass = 0.1
mean_porosity = 0.7
MESH = pl.DeviceIdType.MESH
F32 = jnp.float32
BF16 = jnp.bfloat16
MOVES = [(1, 0), (-1, 0), (0, 1), (0, -1), (1, 1), (1, -1), (-1, 1), (-1, -1)]
PLAIN = 48


def legendre_columns(node_set, degree):
    table = [node_set * 0.0 + 1.0, node_set]
    for order in range(2, degree + 1):
        table.append(((2 * order - 1) * node_set * table[order - 1] - (order - 1) * table[order - 2]) / order)
    return table


def gll_tables():
    degree = N - 1
    node_set = np.cos(math.pi * np.arange(degree + 1) / degree)
    for _ in range(100):
        table = legendre_columns(node_set, degree)
        node_set = node_set - (node_set * table[degree] - table[degree - 1]) / ((degree + 1) * table[degree])
    node_set = node_set[::-1].copy()
    values = legendre_columns(node_set, degree)[degree]
    weights = 2.0 / (degree * (degree + 1) * values**2)
    derivative = np.zeros((N, N))
    for a in range(N):
        for b in range(N):
            if a != b:
                derivative[a, b] = values[a] / (values[b] * (node_set[a] - node_set[b]))
    derivative[0, 0] = -degree * (degree + 1) / 4.0
    derivative[N - 1, N - 1] = degree * (degree + 1) / 4.0
    return weights, derivative


def schwarz_tables():
    weights, derivative = gll_tables()
    stiffness = derivative.T @ (weights[:, None] * derivative)
    total = 3 * (N - 1) + 1
    three_stiffness = np.zeros((total, total))
    three_mass = np.zeros(total)
    for element in range(3):
        at = element * (N - 1)
        three_stiffness[at : at + N, at : at + N] += stiffness
        three_mass[at : at + N] += weights
    chosen = np.array([N - 2] + list(range(N - 1, 2 * N - 1)) + [2 * N - 1])
    scaling = 1.0 / np.sqrt(three_mass[chosen])
    symmetric = scaling[:, None] * three_stiffness[chosen][:, chosen] * scaling[None, :]
    values, vectors = np.linalg.eigh(0.5 * (symmetric + symmetric.T))
    return scaling[:, None] * vectors, values


def hi_lo(matrix):
    high = matrix.astype(ml_dtypes.bfloat16)
    low = (matrix - high.astype(np.float64)).astype(ml_dtypes.bfloat16)
    return np.concatenate([high, low], axis=-2)


def schwarz_blocks():
    basis, values = schwarz_tables()
    m = N + 2
    divisor = mean_porosity * (values[:, None, None] + values[None, :, None] + values[None, None, :]) + shift_mass
    fold = np.zeros((2, m // 2, m))
    for i in range(m // 2):
        fold[0, i, i] = fold[0, i, m - 1 - i] = 1.0
        fold[1, i, i], fold[1, i, m - 1 - i] = 1.0, -1.0
    order = np.zeros((m // 2, m // 2, m), np.int64)
    for i in range(m // 2):
        for j in range(m // 2):
            at = i * (m // 2) + j
            order[i, j, 1 : m - 1] = at * N + np.arange(N)
            order[i, j, 0] = (m // 2) ** 2 * N + at
            order[i, j, m - 1] = (m // 2) ** 2 * (N + 1) + at
    order = order.reshape(-1)
    blocks = np.zeros((4, 256, 256))
    for p in range(2):
        for q in range(2):
            left = np.kron(np.kron(fold[p] @ basis, fold[q] @ basis), basis)
            block = (left / divisor.reshape(-1)) @ left.T / 16.0
            blocks[2 * p + q][np.ix_(order, order)] = block
    return hi_lo(blocks)


def stiffness_blocks():
    weights, derivative = gll_tables()
    one = derivative.T @ (weights[:, None] * derivative)
    mass = np.diag(weights)
    whole = (
        np.kron(np.kron(one, mass), mass) + np.kron(np.kron(mass, one), mass) + np.kron(np.kron(mass, mass), one)
    )
    half = N // 2 * N * N
    blocks = np.zeros((2, half, half))
    for p, sign in enumerate((1.0, -1.0)):
        fold = np.zeros((N // 2, N))
        for i in range(N // 2):
            fold[i, i], fold[i, N - 1 - i] = 1.0, sign
        fold = np.kron(fold, np.eye(N * N))
        blocks[p] = fold @ whole @ fold.T / 4.0
    return hi_lo(blocks)


def cosine_basis(count):
    position = np.arange(count, dtype=np.float64)
    phase = math.pi * (position[:, None] + 0.5) * position[None, :] / count
    norm = np.where(position == 0, math.sqrt(1.0 / count), math.sqrt(2.0 / count))
    return np.cos(phase) * norm[None, :], 2.0 - 2.0 * np.cos(math.pi * position / count)


def share_rows(count):
    table = np.zeros((count, 3, count))
    for at in range(count):
        table[at, :, at] = 1.0
        if at > 0:
            table[at, 0, at], table[at, 0, at - 1] = 0.5, 0.5
        if at < count - 1:
            table[at, 2, at], table[at, 2, at + 1] = 0.5, 0.5
    return table


def coarse_tables(nx, ny, length):
    first, eigen_first = cosine_basis(nx)
    second, eigen_second = cosine_basis(ny)
    divisor = (
        2.0 * mean_porosity * length * (eigen_first[:, None] + eigen_second[None, :]) + 8.0 * shift_mass * length
    )
    share_first, share_second = share_rows(nx), share_rows(ny)
    along_y = np.ones((ny, 128))
    along_x = np.ones((nx, nx, 128))
    green = np.einsum("ap,bp,pk->kab", first, first, 1.0 / divisor)
    back = np.zeros((ny, 16, 128))
    for t in range(3):
        lanes = slice(t * ny, (t + 1) * ny)
        along_y[:, lanes] = second
        along_x[:, :, lanes] = np.einsum("xc,kcb->xbk", share_first[:, t], green)
        for s in range(3):
            back[:, 3 * t + s, lanes] = share_second[:, s] @ second
    for row in range(3):
        back[:, 9 + row, PLAIN + 16 * row] = 1.0
    return along_y.astype(np.float32), along_x.astype(np.float32), back.astype(np.float32)


def mass_table():
    weights, _ = gll_tables()
    table = shift_mass * (weights[:, None] * weights[None, :]).reshape(N * N, 1)
    return np.broadcast_to(table, (N * N, 128)).astype(np.float32).copy()


def part(step, low, high, whole):
    return low if step < 0 else (high if step > 0 else whole)


def span(first, count, unit=1):
    return pl.ds(first * unit, count * unit)


def kernel(
    nx, ny, node_weights,
    sol_in, res_in, grains_in, schwarz_in, stiff_in, along_y_in, along_x_in, back_in, mass_in,
    sol_out, res_out, dir_out, steps_out,
    sol, ext0, ext1, grains, schwarz, stiff, along_y, along_x, back, mass,
    blk, oblk, ab, loc0, loc1, d, w, q1, qw, lift, msg, buf_y, buf_x, sv, sides, corners, sides1, corners1,
    z2, r1, im2,
    load_sem, send_sem, recv_sem, gy_send, gy_recv, gx_send, gx_recv,
):
    x, y = lax.axis_index("gx"), lax.axis_index("gy")

    def inside(dx, dy):
        checks = []
        if dx > 0:
            checks.append(x < nx - 1)
        if dx < 0:
            checks.append(x > 0)
        if dy > 0:
            checks.append(y < ny - 1)
        if dy < 0:
            checks.append(y > 0)
        return functools.reduce(jnp.logical_and, checks)

    loads = [
        pltpu.make_async_copy(src, dst, load_sem.at[i])
        for i, (src, dst) in enumerate(
            [
                (res_in.at[0, 0], ext0.at[pl.ds(1, N), pl.ds(N, N * N)]),
                (schwarz_in, schwarz),
                (along_y_in, along_y),
                (along_x_in.at[x], along_x),
                (back_in.at[y], back),
                (grains_in.at[0], grains),
                (stiff_in, stiff),
                (mass_in, mass),
                (sol_in.at[0, 0], sol),
            ]
        )
    ]
    for load in loads:
        load.start()

    for m, (dx, dy) in enumerate(MOVES):

        @pl.when(jnp.logical_not(inside(-dx, -dy)))
        def _():
            for phase in range(3):
                incoming(sides, corners, phase, m)[...] = jnp.zeros_like(incoming(sides, corners, phase, m))
            edge = incoming(sides1, corners1, None, m)
            edge[...] = jnp.zeros_like(edge)
            area = ext0.at[span(*part(dx, (N + 1, 1), (0, 1), (1, N))), span(*part(dy, (N + 1, 1), (0, 1), (1, N)), N)]
            area[...] = jnp.zeros_like(area)

    barrier = pltpu.get_barrier_semaphore()

    @pl.loop(1, ny)
    def _(k):
        pl.semaphore_signal(barrier, inc=1, device_id=(x, lax.rem(y + k, ny)), device_id_type=MESH)

    @pl.loop(1, nx)
    def _(k):
        pl.semaphore_signal(barrier, inc=1, device_id=(lax.rem(x + k, nx), y), device_id_type=MESH)

    expected = jnp.int32(nx - 1 + ny - 1)
    for dx, dy in MOVES:
        if dx and dy:
            there = inside(dx, dy)
            expected = expected + there.astype(jnp.int32)

            @pl.when(there)
            def _():
                pl.semaphore_signal(barrier, inc=1, device_id=(x + dx, y + dy), device_id_type=MESH)

    pl.semaphore_wait(barrier, expected)

    def copies(phase, source, target):
        return [
            pltpu.make_async_remote_copy(
                src_ref=source(dx, dy),
                dst_ref=target(m),
                send_sem=send_sem.at[phase, m],
                recv_sem=recv_sem.at[phase, m],
                device_id=(x + dx, y + dy),
                device_id_type=MESH,
            )
            for m, (dx, dy) in enumerate(MOVES)
        ]

    def start(group):
        for m, (dx, dy) in enumerate(MOVES):
            pl.when(inside(dx, dy))(group[m].start)

    def arrive(group):
        for m, (dx, dy) in enumerate(MOVES):
            pl.when(inside(-dx, -dy))(group[m].wait_recv)

    def sent(group):
        for m, (dx, dy) in enumerate(MOVES):
            pl.when(inside(dx, dy))(group[m].wait_send)

    def ext_target(m):
        dx, dy = MOVES[m]
        return ext0.at[span(*part(dx, (N + 1, 1), (0, 1), (1, N))), span(*part(dy, (N + 1, 1), (0, 1), (1, N)), N)]

    halo0 = copies(
        0,
        lambda dx, dy: res_in.at[
            0, 0, span(*part(dx, (1, 1), (N - 2, 1), (0, N))), span(*part(dy, (1, 1), (N - 2, 1), (0, N)), N)
        ],
        ext_target,
    )
    start(halo0)

    lane = lax.broadcasted_iota(jnp.int32, (1, 128), 1)
    last = 127
    row = lax.broadcasted_iota(jnp.int32, (N * N, 128), 0)
    wide = lax.broadcasted_iota(jnp.int32, (N * N, 128), 1)
    inner = lax.rem(row, N)
    shared_z = ((inner == 0) & (wide > 0)) | ((inner == N - 1) & (wide < last))
    weight_z = jnp.where(shared_z, 0.5, 1.0).astype(F32)
    low_y = jnp.where(y > 0, 0.5, 1.0).astype(F32)
    high_y = jnp.where(y < ny - 1, 0.5, 1.0).astype(F32)
    low_x = jnp.where(x > 0, 0.5, 1.0).astype(F32)
    high_x = jnp.where(x < nx - 1, 0.5, 1.0).astype(F32)
    weight_yz = weight_z * jnp.where(row < N, low_y, jnp.where(row >= N * N - N, high_y, 1.0))

    def from_below(v):
        return jnp.where(lane > 0, pltpu.roll(v, 1, axis=1), 0.0)

    def from_above(v):
        return jnp.where(lane < last, pltpu.roll(v, last, axis=1), 0.0)

    def total(v):
        return jnp.sum(jnp.sum(v, axis=0, keepdims=True), axis=1, keepdims=True)

    def weighted(product):
        middle = product(1)
        for a in range(2, N - 1):
            middle = middle + product(a)
        return total(weight_yz * (low_x * product(0) + middle + high_x * product(N - 1)))

    own = pl.ds(N, N * N)

    def stage(buffer, index, send, recv, count, device):
        def copy(k):
            return pltpu.make_async_remote_copy(
                src_ref=buffer.at[pl.ds(index, 1)],
                dst_ref=buffer.at[pl.ds(index, 1)],
                send_sem=send,
                recv_sem=recv,
                device_id=device(k),
                device_id_type=MESH,
            )

        @pl.loop(1, count)
        def _(k):
            copy(k).start()

    def all_rows(buffer, send, recv, count):
        rows = buffer.at[pl.ds(0, count - 1)]
        pltpu.make_async_copy(rows, rows, recv).wait()
        pltpu.make_async_copy(rows, rows, send).wait()

    def gather_y(g, value):
        buf_y[g, pl.ds(y, 1)] = value.reshape(1, 1, 128)
        stage(buf_y.at[g], y, gy_send.at[g], gy_recv.at[g], ny, lambda k: (x, lax.rem(y + k, ny)))

    def gather_x(g):
        all_rows(buf_y.at[g], gy_send.at[g], gy_recv.at[g], ny)
        value = jnp.sum(buf_y[g].reshape(ny, 128) * along_y[...], axis=0, keepdims=True)
        buf_x[g, pl.ds(x, 1)] = value.reshape(1, 1, 128)
        stage(buf_x.at[g], x, gx_send.at[g], gx_recv.at[g], nx, lambda k: (lax.rem(x + k, nx), y))

    def gathered(g):
        all_rows(buf_x.at[g], gx_send.at[g], gx_recv.at[g], nx)
        value = jnp.sum(buf_x[g].reshape(nx, 128) * along_x[...], axis=0, keepdims=True)
        sums = jnp.sum(value * back[...], axis=1, keepdims=True)
        sv[g] = jnp.broadcast_to(sums, (16, 128))

    def lifted(g):
        for t in range(3):
            for s in range(3):
                at, count = ((0, 1), (1, N - 2), (N - 1, 1))[s]
                lift[t, pl.ds(at * N, count * N)] = jnp.broadcast_to(sv[g, pl.ds(3 * t + s, 1)], (count * N, 128))

    def message(*values):
        result = values[0]
        for i, value in enumerate(values[1:]):
            result = jnp.where(lane < PLAIN + 16 * i, result, value)
        return jnp.broadcast_to(result, (1, 128))

    def product(matrix, v):
        high = v.astype(BF16)
        low = (v - high.astype(F32)).astype(BF16)
        out = jnp.dot(matrix, jnp.concatenate([high, low], axis=1), preferred_element_type=F32)
        half = matrix.shape[0] // 2
        return (out[half:, :128] + out[:half, 128:]) + out[:half, :128]

    def solve(ext, loc):
        h = (N + 2) // 2
        for i in range(h):
            lower, upper = ext[i], ext[N + 1 - i]
            even, odd = lower + upper, lower - upper
            for j in range(h):
                one, two = slice(j * N, j * N + N), slice((N + 1 - j) * N, (N + 2 - j) * N)
                at = pl.ds((i * h + j) * N, N)
                blk[0, at] = even[one] + even[two]
                blk[1, at] = even[one] - even[two]
                blk[2, at] = odd[one] + odd[two]
                blk[3, at] = odd[one] - odd[two]
        count = h * h

        @pl.loop(0, 4)
        def _(p):
            source, out = blk.at[p], oblk.at[p]
            below = source[pl.ds(N - 2, count, stride=N)]
            above = source[pl.ds(1, count, stride=N)]
            source[pl.ds(count * N, count)] = from_below(below)
            source[pl.ds(count * (N + 1), count)] = from_above(above)
            out[...] = product(schwarz[p], source[...])
            first = out[pl.ds(0, count, stride=N)]
            final = out[pl.ds(N - 1, count, stride=N)]
            out[pl.ds(0, count, stride=N)] = first + from_below(final)
            out[pl.ds(N - 1, count, stride=N)] = final + from_above(first)
            out[pl.ds(1, count, stride=N)] += from_below(out[pl.ds(count * (N + 1), count)])
            out[pl.ds(N - 2, count, stride=N)] += from_above(out[pl.ds(count * N, count)])

        for i in range(h):
            for j in range(h):
                at = pl.ds((i * h + j) * N, N)
                ee, eo, oe, oo = oblk[0, at], oblk[1, at], oblk[2, at], oblk[3, at]
                one, two = pl.ds(j * N, N), pl.ds((N + 1 - j) * N, N)
                loc[i, one] = (ee + eo) + (oe + oo)
                loc[N + 1 - i, one] = (ee + eo) - (oe + oo)
                loc[i, two] = (ee - eo) + (oe - oo)
                loc[N + 1 - i, two] = (ee - eo) - (oe - oo)

    def spread_copies(phase, slot, loc):
        return copies(
            phase,
            lambda dx, dy: loc.at[
                span(*part(dx, (0, 2), (N, 2), (1, N))), span(*part(dy, (0, 2), (N, 2), (1, N)), N)
            ],
            lambda m: incoming(sides, corners, slot, m),
        )

    def add_nodes(field, slot):
        for m, (dx, dy) in enumerate(MOVES):
            area = field.at[
                span(*part(dx, (N - 2, 2), (0, 2), (0, N))), span(*part(dy, (N - 2, 2), (0, 2), (0, N)), N)
            ]
            area[...] += incoming(sides, corners, slot, m)[...]

    def combine(field, loc):
        for a in range(N):
            field[a] = loc[a + 1, own] + lift[0 if a == 0 else (2 if a == N - 1 else 1)]

    porosity = None

    def apply(field, image):
        for a in range(N // 2):
            lower, upper = field[a], field[N - 1 - a]
            ab[0, pl.ds(a * N * N, N * N)] = lower + upper
            ab[1, pl.ds(a * N * N, N * N)] = lower - upper
        even = product(stiff[0], ab[0])
        odd = product(stiff[1], ab[1])
        for a in range(N // 2):
            at = slice(a * N * N, (a + 1) * N * N)
            scaled = mass[...] * F32(node_weights[a])
            image[a] = porosity * (even[at] + odd[at]) + scaled * field[a]
            image[N - 1 - a] = porosity * (even[at] - odd[at]) + scaled * field[N - 1 - a]
        for a in range(N):
            first = image[a, pl.ds(0, N, stride=N)]
            final = image[a, pl.ds(N - 1, N, stride=N)]
            image[a, pl.ds(0, N, stride=N)] = first + from_below(final)
            image[a, pl.ds(N - 1, N, stride=N)] = final + from_above(first)

    loads[0].wait()
    coarse0 = weighted(lambda a: ext0[a + 1, own])
    gather_y(0, message(coarse0))
    for p in range(4):
        blk[p, pl.ds(248, 8)] = jnp.zeros((8, 128), F32)
    for load in loads[1:]:
        load.wait()
    porosity = 1.0 - 0.6 * grains[...].astype(F32) / MOST_GRAINS
    gather_x(0)
    arrive(halo0)
    solve(ext0, loc0)
    spread0 = spread_copies(1, 0, loc0)
    start(spread0)
    gathered(0)
    lifted(0)
    combine(d, loc0)
    arrive(spread0)
    add_nodes(d, 0)

    apply(d, q1)
    faces = copies(
        2,
        lambda dx, dy: q1.at[
            span(*part(dx, (0, 2), (N - 2, 2), (0, N))), span(*part(dy, (0, 2), (N - 2, 2), (0, N)), N)
        ],
        lambda m: incoming(sides, corners, 1, m),
    )
    start(faces)
    rho1 = weighted(lambda a: ext0[a + 1, own] * d[a])
    curve = d[0] * q1[0]
    for a in range(1, N):
        curve = curve + d[a] * q1[a]
    curve1 = total(weight_z * curve)
    for i in (0, N + 1):
        ext1[i] = jnp.zeros_like(ext1[i])
    for a in range(N):
        ext1[a + 1, pl.ds(0, N)] = jnp.zeros((N, 128), F32)
        ext1[a + 1, own] = q1[a]
        ext1[a + 1, pl.ds(N * N + N, N)] = jnp.zeros((N, 128), F32)
    arrive(faces)
    for m, (dx, dy) in enumerate(MOVES):
        area = ext1.at[span(*part(dx, (N, 2), (0, 2), (1, N))), span(*part(dy, (N, 2), (0, 2), (1, N)), N)]
        area[...] += incoming(sides, corners, 1, m)[...]

    coarse1 = weighted(lambda a: ext1[a + 1, own])
    gather_y(1, message(coarse1, rho1, curve1))
    solve(ext1, loc1)
    spread1 = spread_copies(3, 2, loc1)
    start(spread1)
    gather_x(1)
    gathered(1)
    lifted(1)
    combine(w, loc1)
    arrive(spread1)
    add_nodes(w, 2)

    apply(w, qw)
    edges = copies(
        4,
        lambda dx, dy: qw.at[
            span(*part(dx, (0, 1), (N - 1, 1), (0, N))), span(*part(dy, (0, 1), (N - 1, 1), (0, N)), N)
        ],
        lambda m: incoming(sides1, corners1, None, m),
    )
    start(edges)
    rho1, curve1 = sv[1, pl.ds(9, 1)], sv[1, pl.ds(10, 1)]
    step1 = rho1 / curve1
    curve_new, curve_mixed = None, None
    for a in range(N):
        z_a = d[a] - step1 * w[a]
        z2[a] = z_a
        r1[a] = ext0[a + 1, own] - step1 * ext1[a + 1, own]
        new = z_a * (q1[a] - step1 * qw[a])
        mixed = z_a * q1[a]
        curve_new = new if a == 0 else curve_new + new
        curve_mixed = mixed if a == 0 else curve_mixed + mixed
    rho2 = weighted(lambda a: r1[a] * z2[a])
    gather_y(2, message(rho2, rho2, total(weight_z * curve_new), total(weight_z * curve_mixed)))
    for a in range(N):
        im2[a] = qw[a]
    arrive(edges)
    for m, (dx, dy) in enumerate(MOVES):
        area = im2.at[
            span(*part(dx, (N - 1, 1), (0, 1), (0, N))), span(*part(dy, (N - 1, 1), (0, 1), (0, N)), N)
        ]
        area[...] += incoming(sides1, corners1, None, m)[...]
    gather_x(2)
    for a in range(N):
        im2[a] = ext1[a + 1, own] - step1 * im2[a]
        sol[a] = sol[a] + step1 * d[a]
    gathered(2)
    rho2, curve_new, curve_mixed = sv[2, pl.ds(9, 1)], sv[2, pl.ds(10, 1)], sv[2, pl.ds(11, 1)]
    ratio = rho2 / rho1
    step2 = rho2 / (curve_new + ratio * (2.0 * curve_mixed + ratio * curve1))
    for a in range(N):
        direction = z2[a] + ratio * d[a]
        dir_out[0, 0, a] = direction
        sol_out[0, 0, a] = sol[a] + step2 * direction
        res_out[0, 0, a] = r1[a] - step2 * (im2[a] + ratio * ext1[a + 1, own])
    steps_out[0] = step1[0, 0]
    steps_out[1] = step2[0, 0]
    for group in (halo0, spread0, faces, spread1, edges):
        sent(group)


def incoming(sides, corners, slot, m):
    first, second = MOVES[m]
    if first and second:
        return corners.at[m - 4] if slot is None else corners.at[slot, m - 4]
    which = 0 if first else 1
    ref = sides[which]
    return ref.at[m % 2] if slot is None else ref.at[slot, m % 2]


def solution(mesh):
    nx, ny = mesh.shape["gx"], mesh.shape["gy"]
    weights, _ = gll_tables()
    along_y, along_x, back = coarse_tables(nx, ny, 128)
    schwarz, stiff, mass = schwarz_blocks(), stiffness_blocks(), mass_table()
    nn = N * N
    field = pltpu.VMEM((N, nn, 128), F32)
    wide = pltpu.VMEM((N + 2, nn + 2 * N, 128), F32)
    vmem, anywhere = pl.BlockSpec(memory_space=pltpu.VMEM), pl.BlockSpec(memory_space=pl.ANY)
    smem = pl.BlockSpec(memory_space=pltpu.SMEM)

    def step(sol, res, grains):
        shape = sol.shape
        flat = (1, 1, N, nn, 128)
        out = jax.ShapeDtypeStruct(flat, F32)
        outs = pl.pallas_call(
            functools.partial(kernel, nx, ny, [float(v) for v in weights]),
            out_shape=(out, out, out, jax.ShapeDtypeStruct((2,), F32)),
            in_specs=[anywhere] * 9,
            out_specs=(vmem, vmem, vmem, smem),
            scratch_shapes=[
                field, wide, wide,
                pltpu.VMEM((1, 128), jnp.int32),
                pltpu.VMEM((4, 512, 256), BF16),
                pltpu.VMEM((2, 512, 256), BF16),
                pltpu.VMEM((ny, 128), F32),
                pltpu.VMEM((nx, 128), F32),
                pltpu.VMEM((16, 128), F32),
                pltpu.VMEM((nn, 128), F32),
                pltpu.VMEM((4, 256, 128), F32),
                pltpu.VMEM((4, 256, 128), F32),
                pltpu.VMEM((2, 256, 128), F32),
                wide, wide, field, field, field, field,
                pltpu.VMEM((3, nn, 128), F32),
                pltpu.VMEM((8, 128), F32),
                pltpu.VMEM((3, ny, 1, 128), F32),
                pltpu.VMEM((3, nx, 1, 128), F32),
                pltpu.VMEM((3, 16, 128), F32),
                [pltpu.VMEM((3, 2, 2, nn, 128), F32), pltpu.VMEM((3, 2, N, 2 * N, 128), F32)],
                pltpu.VMEM((3, 4, 2, 2 * N, 128), F32),
                [pltpu.VMEM((2, 1, nn, 128), F32), pltpu.VMEM((2, N, N, 128), F32)],
                pltpu.VMEM((4, 1, N, 128), F32),
                field, field, field,
                pltpu.SemaphoreType.DMA((9,)),
                pltpu.SemaphoreType.DMA((5, 8)),
                pltpu.SemaphoreType.DMA((5, 8)),
                pltpu.SemaphoreType.DMA((3,)),
                pltpu.SemaphoreType.DMA((3,)),
                pltpu.SemaphoreType.DMA((3,)),
                pltpu.SemaphoreType.DMA((3,)),
            ],
            compiler_params=pltpu.CompilerParams(
                collective_id=0, has_side_effects=True, vmem_limit_bytes=40 * 1024 * 1024
            ),
            name="cg_steps",
        )(
            sol.reshape(flat), res.reshape(flat), grains,
            jnp.asarray(schwarz), jnp.asarray(stiff), jnp.asarray(along_y), jnp.asarray(along_x),
            jnp.asarray(back), jnp.asarray(mass),
        )
        return tuple(v.reshape(shape) for v in outs[:3]) + (outs[3],)

    wide_spec = P("gx", "gy", None, None, None, None)
    return jax.shard_map(
        step,
        mesh=mesh,
        in_specs=(wide_spec, wide_spec, P("gx", "gy", None)),
        out_specs=(wide_spec, wide_spec, wide_spec, P()),
        check_vma=False,
    )
```

time: 665 us -> 68.4 us (0.10)
  blocking collectives: 516 us -> 0 us
  Pallas kernels: 0 us -> 56.4 us
  starting transfers between devices: 56.1 us -> 0 us
  waiting for transfers between devices: 41.3 us -> 0 us
  matrix products: 21.7 us -> 0 us
  other arithmetic: 8.98 us -> 0 us
    psum x5 -> x0, blocking collectives: 516 us -> none  [the longest x2 209 us: shards(): lax.psum(jnp.sum(inverse_all * residual * preconditioned), ('gx', 'gy'))]
    pallas_call x0 -> x1, Pallas kernels: none -> 56.4 us  [step(): pl.pallas_call(functools.partial(kernel, nx, ny, [float(v) for v in weigh...]
    ppermute x24 -> x0, starting transfers between devices: 56.1 us -> none  [the longest x12 36.4 us: padded_2(): lax.ppermute(lax.slice_in_dim(block, block.shape[dim] - width, None, axis...]
    ppermute x24 -> x0, waiting for transfers between devices: 41.3 us -> none  [the longest x12 41.2 us: padded_2(): lax.ppermute(lax.slice_in_dim(block, 0, width, axis=dim), axis, backward)]
    dot_general x40 -> x0, matrix products: 21.7 us -> none  [the longest x2 2.4 us: schwarz_solve(): jnp.einsum('jb,...ibce->...ijce', eigen_basis, back_first, precision=exac...]
  transfers between devices with their start and end apart: 24 -> 0, of which waited for: 11 -> 0; matrix products, arithmetic and copies ran while one was open for 1% -> 0% of each run, Pallas kernels for 0% -> 0%
where the time goes in v1:
time: 68.4 us; the launch traced here: 67.9 us
  Pallas kernels  56.4 us (82%)
  local copies, waits for them, and re-layouts  10.8 us (16%)
    pallas_call x1, Pallas kernels, step(): pl.pallas_call(functools.partial(kernel, nx, ny, [float(v) for v in weigh...  56.4 us
    unnamed x22, local copies, waits for them, and re-layouts  10.8 us

profile of v1, /device:TPU:1, one launch (start us, length us, event | category | flops | bytes accessed | tf_op | source)
XLA Modules:
  0.0 67.9 jit_solution(1001162157052238520)
XLA Ops:
  0.6 0.0 copy-start.8
  0.6 0.6 copy-done.8
  1.3 0.0 copy-start
  1.3 1.2 %copy-done = bf16[4,512,256]{2,1,0:T(8,128)(2,1)S(1)} copy-done((bf16[4,512,256]{2,1,0:T(8,128)(2,1)S(1)}, bf16[4,512,256]{2,1,0:T(8,128)(2,1)}, u32[]{:S(2)}) %copy-start) | copy-done | bytes 1048600
  2.5 0.0 copy-start.1
  2.5 1.0 %copy-done.1 = f32[32,32,128]{2,1,0:T(8,128)S(1)} copy-done((f32[32,32,128]{2,1,0:T(8,128)S(1)}, f32[32,32,128]{2,1,0:T(8,128)}, u32[]{:S(2)}) %copy-start.1) | copy-done | bytes 524312
  3.6 0.0 copy-start.2
  3.6 1.0 %copy-done.2 = bf16[2,512,256]{2,1,0:T(8,128)(2,1)S(1)} copy-done((bf16[2,512,256]{2,1,0:T(8,128)(2,1)S(1)}, bf16[2,512,256]{2,1,0:T(8,128)(2,1)}, u32[]{:S(2)}) %copy-start.2) | copy-done | bytes 524312
  4.6 0.0 copy-start.3
  4.6 0.9 %copy-done.3 = f32[1,1,8,8,8,128]{5,4,3,2,1,0:T(8,128)S(1)} copy-done((f32[1,1,8,8,8,128]{5,4,3,2,1,0:T(8,128)S(1)}, f32[1,1,8,8,8,128]{5,4,3,2,1,0:T(8,128)}, u32[]{:S(2)}) %copy-start.3) | copy-done | bytes 262168
  5.5 0.0 copy-start.4
  5.5 0.9 %copy-done.4 = f32[1,1,8,8,8,128]{5,4,3,2,1,0:T(8,128)S(1)} copy-done((f32[1,1,8,8,8,128]{5,4,3,2,1,0:T(8,128)S(1)}, f32[1,1,8,8,8,128]{5,4,3,2,1,0:T(8,128)}, u32[]{:S(2)}) %copy-start.4) | copy-done | bytes 262168
  6.5 0.0 copy-start.5
  6.5 0.9 %copy-done.5 = f32[16,16,128]{2,1,0:T(8,128)S(1)} copy-done((f32[16,16,128]{2,1,0:T(8,128)S(1)}, f32[16,16,128]{2,1,0:T(8,128)}, u32[]{:S(2)}) %copy-start.5) | copy-done | bytes 131096
  7.4 0.0 copy-start.6
  7.4 0.8 %copy-done.6 = f32[64,128]{1,0:T(8,128)S(1)} copy-done((f32[64,128]{1,0:T(8,128)S(1)}, f32[64,128]{1,0:T(8,128)}, u32[]{:S(2)}) %copy-start.6) | copy-done | bytes 32792
  8.2 0.0 copy-start.7
  8.2 0.7 %copy-done.7 = f32[16,128]{1,0:T(8,128)S(1)} copy-done((f32[16,128]{1,0:T(8,128)S(1)}, f32[16,128]{1,0:T(8,128)}, u32[]{:S(2)}) %copy-start.7) | copy-done | bytes 8216
  8.9 56.4 %cg_steps.1 = (f32[1,1,8,64,128]{4,3,2,1,0:T(8,128)S(1)}, f32[1,1,8,64,128]{4,3,2,1,0:T(8,128)S(1)}, f32[1,1,8,64,128]{4,3,2,1,0:T(8,128)S(1)}, f32[2]{0:T(128)S(1)}) custom-call(f32[1,1,8,64,128]{4,3,2,1,0:T(8,128)S(1)} %bitcast.5, f32[1,1,8,64,128]{4,3,2,1,0:T(8,128)S(1)} %bitcast.6, s32[1,1,128]{2,1,0:T(1,128)S(1)} %copy-done.8, ...), custom_call_target="tpu_custom_call" | custom-call | tf_op jit(solution)/shard_map/cg_steps/pallas_call | solution.py:576
  65.3 0.7 %copy.17 = f32[1,1,8,8,8,128]{5,4,3,2,1,0:T(8,128)} copy(f32[1,1,8,8,8,128]{5,4,3,2,1,0:T(8,128)S(1)} %bitcast.9) | data formatting | bytes 524288
  66.0 0.7 %copy.18 = f32[1,1,8,8,8,128]{5,4,3,2,1,0:T(8,128)} copy(f32[1,1,8,8,8,128]{5,4,3,2,1,0:T(8,128)S(1)} %bitcast.8) | data formatting | bytes 524288
  66.7 0.7 %copy.19 = f32[1,1,8,8,8,128]{5,4,3,2,1,0:T(8,128)} copy(f32[1,1,8,8,8,128]{5,4,3,2,1,0:T(8,128)S(1)} %bitcast.7) | data formatting | bytes 524288
  67.4 0.5 copy.20
Async XLA Ops:
  0.6 0.7 copy-start.8
  1.3 1.2 %copy-start = (bf16[4,512,256]{2,1,0:T(8,128)(2,1)S(1)}, bf16[4,512,256]{2,1,0:T(8,128)(2,1)}, u32[]{:S(2)}) copy-start(bf16[4,512,256]{2,1,0:T(8,128)(2,1)} %constant.12.clone.schwarz_in) | copy-start | bytes 3145732
  2.5 1.0 %copy-start.1 = (f32[32,32,128]{2,1,0:T(8,128)S(1)}, f32[32,32,128]{2,1,0:T(8,128)}, u32[]{:S(2)}) copy-start(f32[32,32,128]{2,1,0:T(8,128)} %constant.15.clone.along_x_in) | copy-start | bytes 1572868
  3.6 1.0 %copy-start.2 = (bf16[2,512,256]{2,1,0:T(8,128)(2,1)S(1)}, bf16[2,512,256]{2,1,0:T(8,128)(2,1)}, u32[]{:S(2)}) copy-start(bf16[2,512,256]{2,1,0:T(8,128)(2,1)} %constant.13.clone.stiff_in) | copy-start | bytes 1572868
  4.6 0.9 %copy-start.3 = (f32[1,1,8,8,8,128]{5,4,3,2,1,0:T(8,128)S(1)}, f32[1,1,8,8,8,128]{5,4,3,2,1,0:T(8,128)}, u32[]{:S(2)}) copy-start(f32[1,1,8,8,8,128]{5,4,3,2,1,0:T(8,128)} %param.9) | copy-start | bytes 786436
  5.5 0.9 %copy-start.4 = (f32[1,1,8,8,8,128]{5,4,3,2,1,0:T(8,128)S(1)}, f32[1,1,8,8,8,128]{5,4,3,2,1,0:T(8,128)}, u32[]{:S(2)}) copy-start(f32[1,1,8,8,8,128]{5,4,3,2,1,0:T(8,128)} %param.10) | copy-start | bytes 786436
  6.5 0.9 %copy-start.5 = (f32[16,16,128]{2,1,0:T(8,128)S(1)}, f32[16,16,128]{2,1,0:T(8,128)}, u32[]{:S(2)}) copy-start(f32[16,16,128]{2,1,0:T(8,128)} %constant.16.clone.back_in) | copy-start | bytes 393220
  7.4 0.8 %copy-start.6 = (f32[64,128]{1,0:T(8,128)S(1)}, f32[64,128]{1,0:T(8,128)}, u32[]{:S(2)}) copy-start(f32[64,128]{1,0:T(8,128)} %constant.17.clone.mass_in) | copy-start | bytes 98308
  8.2 0.7 %copy-start.7 = (f32[16,128]{1,0:T(8,128)S(1)}, f32[16,128]{1,0:T(8,128)}, u32[]{:S(2)}) copy-start(f32[16,128]{1,0:T(8,128)} %constant.14.clone.along_y_in) | copy-start | bytes 24580

commit v2 on v1

--- a/solution.py
+++ b/solution.py
@@ -18,6 +18,7 @@
 F32 = jnp.float32
 BF16 = jnp.bfloat16
 MOVES = [(1, 0), (-1, 0), (0, 1), (0, -1), (1, 1), (1, -1), (-1, 1), (-1, -1)]
+LONGEST_FIRST = [4, 5, 6, 7, 0, 1, 2, 3]
 PLAIN = 48
 
 
@@ -138,19 +139,23 @@
         2.0 * mean_porosity * length * (eigen_first[:, None] + eigen_second[None, :]) + 8.0 * shift_mass * length
     )
     share_first, share_second = share_rows(nx), share_rows(ny)
-    along_y = np.ones((ny, 128))
-    along_x = np.ones((nx, nx, 128))
     green = np.einsum("ap,bp,pk->kab", first, first, 1.0 / divisor)
+    send = np.zeros((ny, 16, 128))
     back = np.zeros((ny, 16, 128))
+    along_x = np.ones((nx, 3, nx, 128))
     for t in range(3):
         lanes = slice(t * ny, (t + 1) * ny)
-        along_y[:, lanes] = second
-        along_x[:, :, lanes] = np.einsum("xc,kcb->xbk", share_first[:, t], green)
         for s in range(3):
-            back[:, 3 * t + s, lanes] = share_second[:, s] @ second
+            modes = share_second[:, s] @ second
+            send[:, 3 * t + s, lanes] = modes
+            for other in range(3):
+                back[:, 3 * other + s, lanes] = modes
+        for other in range(3):
+            along_x[:, other, :, lanes] = np.einsum("xc,kcd,bd->xbk", share_first[:, other], green, share_first[:, t])
     for row in range(3):
+        send[:, 9 + row, PLAIN + 16 * row] = 1.0
         back[:, 9 + row, PLAIN + 16 * row] = 1.0
-    return along_y.astype(np.float32), along_x.astype(np.float32), back.astype(np.float32)
+    return send.astype(np.float32), along_x.astype(np.float32), back.astype(np.float32)
 
 
 def mass_table():
@@ -169,11 +174,10 @@
 
 def kernel(
     nx, ny, node_weights,
-    sol_in, res_in, grains_in, schwarz_in, stiff_in, along_y_in, along_x_in, back_in, mass_in,
+    sol_in, res_in, grains_in, schwarz_in, stiff_in, send_in, along_x_in, back_in, mass_in,
     sol_out, res_out, dir_out, steps_out,
-    sol, ext0, ext1, grains, schwarz, stiff, along_y, along_x, back, mass,
-    blk, oblk, ab, loc0, loc1, d, w, q1, qw, lift, msg, buf_y, buf_x, sv, sides, corners, sides1, corners1,
-    z2, r1, im2,
+    sol, ext0, ext1, grains, schwarz, stiff, send_table, along_x, back, mass,
+    blk, oblk, ab, loc0, loc1, d, q1, z2, q2, r1, im2, lift, buf_y, buf_x, sv, sides, corners, sides1, corners1,
     load_sem, send_sem, recv_sem, gy_send, gy_recv, gx_send, gx_recv,
 ):
     x, y = lax.axis_index("gx"), lax.axis_index("gy")
@@ -190,13 +194,33 @@
             checks.append(y > 0)
         return functools.reduce(jnp.logical_and, checks)
 
+    barrier = pltpu.get_barrier_semaphore()
+
+    @pl.loop(1, ny)
+    def _(k):
+        pl.semaphore_signal(barrier, inc=1, device_id=(x, lax.rem(y + k, ny)), device_id_type=MESH)
+
+    @pl.loop(1, nx)
+    def _(k):
+        pl.semaphore_signal(barrier, inc=1, device_id=(lax.rem(x + k, nx), y), device_id_type=MESH)
+
+    expected = jnp.int32(nx - 1 + ny - 1)
+    for dx, dy in MOVES:
+        if dx and dy:
+            there = inside(dx, dy)
+            expected = expected + there.astype(jnp.int32)
+
+            @pl.when(there)
+            def _():
+                pl.semaphore_signal(barrier, inc=1, device_id=(x + dx, y + dy), device_id_type=MESH)
+
     loads = [
         pltpu.make_async_copy(src, dst, load_sem.at[i])
         for i, (src, dst) in enumerate(
             [
                 (res_in.at[0, 0], ext0.at[pl.ds(1, N), pl.ds(N, N * N)]),
                 (schwarz_in, schwarz),
-                (along_y_in, along_y),
+                (send_in.at[y], send_table),
                 (along_x_in.at[x], along_x),
                 (back_in.at[y], back),
                 (grains_in.at[0], grains),
@@ -220,26 +244,61 @@
             area = ext0.at[span(*part(dx, (N + 1, 1), (0, 1), (1, N))), span(*part(dy, (N + 1, 1), (0, 1), (1, N)), N)]
             area[...] = jnp.zeros_like(area)
 
-    barrier = pltpu.get_barrier_semaphore()
-
-    @pl.loop(1, ny)
-    def _(k):
-        pl.semaphore_signal(barrier, inc=1, device_id=(x, lax.rem(y + k, ny)), device_id_type=MESH)
-
-    @pl.loop(1, nx)
-    def _(k):
-        pl.semaphore_signal(barrier, inc=1, device_id=(lax.rem(x + k, nx), y), device_id_type=MESH)
-
-    expected = jnp.int32(nx - 1 + ny - 1)
-    for dx, dy in MOVES:
-        if dx and dy:
-            there = inside(dx, dy)
-            expected = expected + there.astype(jnp.int32)
-
-            @pl.when(there)
-            def _():
-                pl.semaphore_signal(barrier, inc=1, device_id=(x + dx, y + dy), device_id_type=MESH)
-
+    lane = lax.broadcasted_iota(jnp.int32, (1, 128), 1)
+    last = 127
+    row = lax.broadcasted_iota(jnp.int32, (N * N, 128), 0)
+    wide = lax.broadcasted_iota(jnp.int32, (N * N, 128), 1)
+    inner = lax.rem(row, N)
+    shared_z = ((inner == 0) & (wide > 0)) | ((inner == N - 1) & (wide < last))
+    weight_z = jnp.where(shared_z, 0.5, 1.0).astype(F32)
+    low_y = jnp.where(y > 0, 0.5, 1.0).astype(F32)
+    high_y = jnp.where(y < ny - 1, 0.5, 1.0).astype(F32)
+    low_x = jnp.where(x > 0, 0.5, 1.0).astype(F32)
+    high_x = jnp.where(x < nx - 1, 0.5, 1.0).astype(F32)
+    weight_yz = weight_z * jnp.where(row < N, low_y, jnp.where(row >= N * N - N, high_y, 1.0))
+
+    def from_below(v):
+        return jnp.where(lane > 0, pltpu.roll(v, 1, axis=1), 0.0)
+
+    def from_above(v):
+        return jnp.where(lane < last, pltpu.roll(v, last, axis=1), 0.0)
+
+    def total(v):
+        return jnp.sum(jnp.sum(v, axis=0, keepdims=True), axis=1, keepdims=True)
+
+    def weighted(product):
+        middle = product(1)
+        for a in range(2, N - 1):
+            middle = middle + product(a)
+        return weight_yz * (low_x * product(0) + middle + high_x * product(N - 1))
+
+    own = pl.ds(N, N * N)
+
+    def classes(field, weight, ends):
+        middle = field(1)
+        for a in range(2, N - 1):
+            middle = middle + field(a)
+        rows = []
+        for scale, value in zip(ends, (field(0), middle, field(N - 1))):
+            value = value * weight * scale
+            inner_rows = value[N : 2 * N]
+            for b in range(2, N - 1):
+                inner_rows = inner_rows + value[b * N : b * N + N]
+            for part_rows in (value[:N], inner_rows, value[N * N - N :]):
+                rows.append(jnp.sum(part_rows, axis=0, keepdims=True))
+        return rows
+
+    def message(rows, *sums):
+        result = jnp.zeros((1, 128), F32)
+        for i, value in enumerate(rows):
+            result = result + jnp.sum(value, axis=1, keepdims=True) * send_table[pl.ds(i, 1)]
+        for i, value in enumerate(sums):
+            result = result + total(value) * send_table[pl.ds(9 + i, 1)]
+        return result
+
+    loads[0].wait()
+    loads[2].wait()
+    first_message = message(classes(lambda a: ext0[a + 1, own], weight_yz, (low_x, 1.0, high_x)))
     pl.semaphore_wait(barrier, expected)
 
     def copies(phase, source, target):
@@ -256,8 +315,8 @@
         ]
 
     def start(group):
-        for m, (dx, dy) in enumerate(MOVES):
-            pl.when(inside(dx, dy))(group[m].start)
+        for m in LONGEST_FIRST:
+            pl.when(inside(*MOVES[m]))(group[m].start)
 
     def arrive(group):
         for m, (dx, dy) in enumerate(MOVES):
@@ -278,37 +337,6 @@
         ],
         ext_target,
     )
-    start(halo0)
-
-    lane = lax.broadcasted_iota(jnp.int32, (1, 128), 1)
-    last = 127
-    row = lax.broadcasted_iota(jnp.int32, (N * N, 128), 0)
-    wide = lax.broadcasted_iota(jnp.int32, (N * N, 128), 1)
-    inner = lax.rem(row, N)
-    shared_z = ((inner == 0) & (wide > 0)) | ((inner == N - 1) & (wide < last))
-    weight_z = jnp.where(shared_z, 0.5, 1.0).astype(F32)
-    low_y = jnp.where(y > 0, 0.5, 1.0).astype(F32)
-    high_y = jnp.where(y < ny - 1, 0.5, 1.0).astype(F32)
-    low_x = jnp.where(x > 0, 0.5, 1.0).astype(F32)
-    high_x = jnp.where(x < nx - 1, 0.5, 1.0).astype(F32)
-    weight_yz = weight_z * jnp.where(row < N, low_y, jnp.where(row >= N * N - N, high_y, 1.0))
-
-    def from_below(v):
-        return jnp.where(lane > 0, pltpu.roll(v, 1, axis=1), 0.0)
-
-    def from_above(v):
-        return jnp.where(lane < last, pltpu.roll(v, last, axis=1), 0.0)
-
-    def total(v):
-        return jnp.sum(jnp.sum(v, axis=0, keepdims=True), axis=1, keepdims=True)
-
-    def weighted(product):
-        middle = product(1)
-        for a in range(2, N - 1):
-            middle = middle + product(a)
-        return total(weight_yz * (low_x * product(0) + middle + high_x * product(N - 1)))
-
-    own = pl.ds(N, N * N)
 
     def stage(buffer, index, send, recv, count, device):
         def copy(k):
@@ -336,13 +364,16 @@
 
     def gather_x(g):
         all_rows(buf_y.at[g], gy_send.at[g], gy_recv.at[g], ny)
-        value = jnp.sum(buf_y[g].reshape(ny, 128) * along_y[...], axis=0, keepdims=True)
+        value = jnp.sum(buf_y[g].reshape(ny, 128), axis=0, keepdims=True)
         buf_x[g, pl.ds(x, 1)] = value.reshape(1, 1, 128)
         stage(buf_x.at[g], x, gx_send.at[g], gx_recv.at[g], nx, lambda k: (lax.rem(x + k, nx), y))
 
     def gathered(g):
         all_rows(buf_x.at[g], gx_send.at[g], gx_recv.at[g], nx)
-        value = jnp.sum(buf_x[g].reshape(nx, 128) * along_x[...], axis=0, keepdims=True)
+        rows = buf_x[g].reshape(nx, 128)
+        low, middle, high = (jnp.sum(rows * along_x[t], axis=0, keepdims=True) for t in range(3))
+        row16 = lax.broadcasted_iota(jnp.int32, (16, 128), 0)
+        value = jnp.where(row16 < 3, low, jnp.where(row16 < 6, middle, high))
         sums = jnp.sum(value * back[...], axis=1, keepdims=True)
         sv[g] = jnp.broadcast_to(sums, (16, 128))
 
@@ -351,12 +382,6 @@
             for s in range(3):
                 at, count = ((0, 1), (1, N - 2), (N - 1, 1))[s]
                 lift[t, pl.ds(at * N, count * N)] = jnp.broadcast_to(sv[g, pl.ds(3 * t + s, 1)], (count * N, 128))
-
-    def message(*values):
-        result = values[0]
-        for i, value in enumerate(values[1:]):
-            result = jnp.where(lane < PLAIN + 16 * i, result, value)
-        return jnp.broadcast_to(result, (1, 128))
 
     def product(matrix, v):
         high = v.astype(BF16)
@@ -413,16 +438,8 @@
             lambda m: incoming(sides, corners, slot, m),
         )
 
-    def add_nodes(field, slot):
-        for m, (dx, dy) in enumerate(MOVES):
-            area = field.at[
-                span(*part(dx, (N - 2, 2), (0, 2), (0, N))), span(*part(dy, (N - 2, 2), (0, 2), (0, N)), N)
-            ]
-            area[...] += incoming(sides, corners, slot, m)[...]
-
-    def combine(field, loc):
-        for a in range(N):
-            field[a] = loc[a + 1, own] + lift[0 if a == 0 else (2 if a == N - 1 else 1)]
+    def node_area(field, dx, dy):
+        return field.at[span(*part(dx, (N - 2, 2), (0, 2), (0, N))), span(*part(dy, (N - 2, 2), (0, 2), (0, N)), N)]
 
     porosity = None
 
@@ -444,13 +461,13 @@
             image[a, pl.ds(0, N, stride=N)] = first + from_below(final)
             image[a, pl.ds(N - 1, N, stride=N)] = final + from_above(first)
 
-    loads[0].wait()
-    coarse0 = weighted(lambda a: ext0[a + 1, own])
-    gather_y(0, message(coarse0))
+    gather_y(0, first_message)
+    start(halo0)
     for p in range(4):
         blk[p, pl.ds(248, 8)] = jnp.zeros((8, 128), F32)
-    for load in loads[1:]:
-        load.wait()
+    for i, load in enumerate(loads):
+        if i not in (0, 2):
+            load.wait()
     porosity = 1.0 - 0.6 * grains[...].astype(F32) / MOST_GRAINS
     gather_x(0)
     arrive(halo0)
@@ -459,11 +476,19 @@
     start(spread0)
     gathered(0)
     lifted(0)
-    combine(d, loc0)
+    for a in range(N):
+        d[a] = loc0[a + 1, own] + lift[0 if a == 0 else (2 if a == N - 1 else 1)]
     arrive(spread0)
-    add_nodes(d, 0)
+    for m, (dx, dy) in enumerate(MOVES):
+        area = node_area(d, dx, dy)
+        area[...] += incoming(sides, corners, 0, m)[...]
 
     apply(d, q1)
+    rho1 = weighted(lambda a: ext0[a + 1, own] * d[a])
+    curve = d[0] * q1[0]
+    for a in range(1, N):
+        curve = curve + d[a] * q1[a]
+    gather_y(1, message(classes(lambda a: q1[a], weight_z, (1.0, 1.0, 1.0)), rho1, weight_z * curve))
     faces = copies(
         2,
         lambda dx, dy: q1.at[
@@ -472,68 +497,61 @@
         lambda m: incoming(sides, corners, 1, m),
     )
     start(faces)
-    rho1 = weighted(lambda a: ext0[a + 1, own] * d[a])
-    curve = d[0] * q1[0]
-    for a in range(1, N):
-        curve = curve + d[a] * q1[a]
-    curve1 = total(weight_z * curve)
     for i in (0, N + 1):
         ext1[i] = jnp.zeros_like(ext1[i])
     for a in range(N):
         ext1[a + 1, pl.ds(0, N)] = jnp.zeros((N, 128), F32)
         ext1[a + 1, own] = q1[a]
         ext1[a + 1, pl.ds(N * N + N, N)] = jnp.zeros((N, 128), F32)
+    gather_x(1)
     arrive(faces)
     for m, (dx, dy) in enumerate(MOVES):
         area = ext1.at[span(*part(dx, (N, 2), (0, 2), (1, N))), span(*part(dy, (N, 2), (0, 2), (1, N)), N)]
         area[...] += incoming(sides, corners, 1, m)[...]
 
-    coarse1 = weighted(lambda a: ext1[a + 1, own])
-    gather_y(1, message(coarse1, rho1, curve1))
     solve(ext1, loc1)
     spread1 = spread_copies(3, 2, loc1)
     start(spread1)
-    gather_x(1)
     gathered(1)
     lifted(1)
-    combine(w, loc1)
+    rho1, curve1 = sv[1, pl.ds(9, 1)], sv[1, pl.ds(10, 1)]
+    step1 = rho1 / curve1
+    for a in range(N):
+        z2[a] = d[a] - step1 * (loc1[a + 1, own] + lift[0 if a == 0 else (2 if a == N - 1 else 1)])
+        r1[a] = ext0[a + 1, own] - step1 * ext1[a + 1, own]
+        sol[a] = sol[a] + step1 * d[a]
     arrive(spread1)
-    add_nodes(w, 2)
-
-    apply(w, qw)
+    for m, (dx, dy) in enumerate(MOVES):
+        area = node_area(z2, dx, dy)
+        area[...] -= step1 * incoming(sides, corners, 2, m)[...]
+
+    apply(z2, q2)
+    curve_new = z2[0] * q2[0]
+    curve_mixed = z2[0] * q1[0]
+    for a in range(1, N):
+        curve_new = curve_new + z2[a] * q2[a]
+        curve_mixed = curve_mixed + z2[a] * q1[a]
+    rho2 = weighted(lambda a: r1[a] * z2[a])
+    gather_y(2, message([], rho2, weight_z * curve_new, weight_z * curve_mixed))
     edges = copies(
         4,
-        lambda dx, dy: qw.at[
+        lambda dx, dy: q2.at[
             span(*part(dx, (0, 1), (N - 1, 1), (0, N))), span(*part(dy, (0, 1), (N - 1, 1), (0, N)), N)
         ],
         lambda m: incoming(sides1, corners1, None, m),
     )
     start(edges)
-    rho1, curve1 = sv[1, pl.ds(9, 1)], sv[1, pl.ds(10, 1)]
-    step1 = rho1 / curve1
-    curve_new, curve_mixed = None, None
     for a in range(N):
-        z_a = d[a] - step1 * w[a]
-        z2[a] = z_a
-        r1[a] = ext0[a + 1, own] - step1 * ext1[a + 1, own]
-        new = z_a * (q1[a] - step1 * qw[a])
-        mixed = z_a * q1[a]
-        curve_new = new if a == 0 else curve_new + new
-        curve_mixed = mixed if a == 0 else curve_mixed + mixed
-    rho2 = weighted(lambda a: r1[a] * z2[a])
-    gather_y(2, message(rho2, rho2, total(weight_z * curve_new), total(weight_z * curve_mixed)))
-    for a in range(N):
-        im2[a] = qw[a]
+        im2[a] = q2[a]
+    gather_x(2)
     arrive(edges)
     for m, (dx, dy) in enumerate(MOVES):
         area = im2.at[
             span(*part(dx, (N - 1, 1), (0, 1), (0, N))), span(*part(dy, (N - 1, 1), (0, 1), (0, N)), N)
         ]
         area[...] += incoming(sides1, corners1, None, m)[...]
-    gather_x(2)
-    for a in range(N):
-        im2[a] = ext1[a + 1, own] - step1 * im2[a]
-        sol[a] = sol[a] + step1 * d[a]
+    for group in (halo0, spread0, faces, spread1, edges):
+        sent(group)
     gathered(2)
     rho2, curve_new, curve_mixed = sv[2, pl.ds(9, 1)], sv[2, pl.ds(10, 1)], sv[2, pl.ds(11, 1)]
     ratio = rho2 / rho1
@@ -545,8 +563,6 @@
         res_out[0, 0, a] = r1[a] - step2 * (im2[a] + ratio * ext1[a + 1, own])
     steps_out[0] = step1[0, 0]
     steps_out[1] = step2[0, 0]
-    for group in (halo0, spread0, faces, spread1, edges):
-        sent(group)
 
 
 def incoming(sides, corners, slot, m):
@@ -561,7 +577,7 @@
 def solution(mesh):
     nx, ny = mesh.shape["gx"], mesh.shape["gy"]
     weights, _ = gll_tables()
-    along_y, along_x, back = coarse_tables(nx, ny, 128)
+    send, along_x, back = coarse_tables(nx, ny, 128)
     schwarz, stiff, mass = schwarz_blocks(), stiffness_blocks(), mass_table()
     nn = N * N
     field = pltpu.VMEM((N, nn, 128), F32)
@@ -583,16 +599,15 @@
                 pltpu.VMEM((1, 128), jnp.int32),
                 pltpu.VMEM((4, 512, 256), BF16),
                 pltpu.VMEM((2, 512, 256), BF16),
-                pltpu.VMEM((ny, 128), F32),
-                pltpu.VMEM((nx, 128), F32),
+                pltpu.VMEM((16, 128), F32),
+                pltpu.VMEM((3, nx, 128), F32),
                 pltpu.VMEM((16, 128), F32),
                 pltpu.VMEM((nn, 128), F32),
                 pltpu.VMEM((4, 256, 128), F32),
                 pltpu.VMEM((4, 256, 128), F32),
                 pltpu.VMEM((2, 256, 128), F32),
-                wide, wide, field, field, field, field,
+                wide, wide, field, field, field, field, field, field,
                 pltpu.VMEM((3, nn, 128), F32),
-                pltpu.VMEM((8, 128), F32),
                 pltpu.VMEM((3, ny, 1, 128), F32),
                 pltpu.VMEM((3, nx, 1, 128), F32),
                 pltpu.VMEM((3, 16, 128), F32),
@@ -600,7 +615,6 @@
                 pltpu.VMEM((3, 4, 2, 2 * N, 128), F32),
                 [pltpu.VMEM((2, 1, nn, 128), F32), pltpu.VMEM((2, N, N, 128), F32)],
                 pltpu.VMEM((4, 1, N, 128), F32),
-                field, field, field,
                 pltpu.SemaphoreType.DMA((9,)),
                 pltpu.SemaphoreType.DMA((5, 8)),
                 pltpu.SemaphoreType.DMA((5, 8)),
@@ -609,13 +623,11 @@
                 pltpu.SemaphoreType.DMA((3,)),
                 pltpu.SemaphoreType.DMA((3,)),
             ],
-            compiler_params=pltpu.CompilerParams(
-                collective_id=0, has_side_effects=True, vmem_limit_bytes=40 * 1024 * 1024
-            ),
+            compiler_params=pltpu.CompilerParams(collective_id=0, has_side_effects=True),
             name="cg_steps",
         )(
             sol.reshape(flat), res.reshape(flat), grains,
-            jnp.asarray(schwarz), jnp.asarray(stiff), jnp.asarray(along_y), jnp.asarray(along_x),
+            jnp.asarray(schwarz), jnp.asarray(stiff), jnp.asarray(send), jnp.asarray(along_x),
             jnp.asarray(back), jnp.asarray(mass),
         )
         return tuple(v.reshape(shape) for v in outs[:3]) + (outs[3],)

time: 68.4 us -> 58.5 us (0.86)
  local copies, waits for them, and re-layouts: 10.8 us -> 5.53 us
  Pallas kernels: 56.4 us -> 52.1 us
    unnamed x22 -> x6, local copies, waits for them, and re-layouts: 10.8 us -> 5.53 us
    pallas_call x1, Pallas kernels: 56.4 us -> 52.1 us  [step(): pl.pallas_call(functools.partial(kernel, nx, ny, [float(v) for v in weigh...]
where the time goes in v2:
time: 58.5 us; the launch traced here: 58.3 us
  Pallas kernels  52.1 us (89%)
  local copies, waits for them, and re-layouts  5.53 us (9%)
  between operations  0.65 us (1%)
    pallas_call x1, Pallas kernels, step(): pl.pallas_call(functools.partial(kernel, nx, ny, [float(v) for v in weigh...  52.1 us
    unnamed x6, local copies, waits for them, and re-layouts  5.53 us

profile of v2, /device:TPU:1, one launch (start us, length us, event | category | flops | bytes accessed | tf_op | source)
XLA Modules:
  0.0 58.3 jit_solution(11584155574666680325)
XLA Ops:
  0.6 52.1 %cg_steps.1 = (f32[1,1,8,64,128]{4,3,2,1,0:T(8,128)}, f32[1,1,8,64,128]{4,3,2,1,0:T(8,128)}, f32[1,1,8,64,128]{4,3,2,1,0:T(8,128)}, f32[2]{0:T(128)}) custom-call(f32[1,1,8,64,128]{4,3,2,1,0:T(8,128)} %bitcast.5, f32[1,1,8,64,128]{4,3,2,1,0:T(8,128)} %bitcast.6, s32[1,1,128]{2,1,0:T(1,128)} %grains_in.1, bf16[4,512,256]{2,1,0:T(8,128)(2,1)} %constant.12.clone.schwarz_in, ...), custom_call_target="tpu_custom_call" | custom-call | tf_op jit(solution)/shard_map/cg_steps/pallas_call | solution.py:592
  52.7 0.0 copy-start
  52.7 1.7 %copy.17 = f32[1,1,8,8,8,128]{5,4,3,2,1,0:T(8,128)} copy(f32[1,1,8,8,8,128]{5,4,3,2,1,0:T(8,128)} %bitcast.9) | data formatting | bytes 524288
  54.4 1.7 %copy.18 = f32[1,1,8,8,8,128]{5,4,3,2,1,0:T(8,128)} copy(f32[1,1,8,8,8,128]{5,4,3,2,1,0:T(8,128)} %bitcast.8) | data formatting | bytes 524288
  56.1 1.7 %copy.19 = f32[1,1,8,8,8,128]{5,4,3,2,1,0:T(8,128)} copy(f32[1,1,8,8,8,128]{5,4,3,2,1,0:T(8,128)} %bitcast.7) | data formatting | bytes 524288
  57.7 0.0 copy-done
  57.7 0.5 copy.20
Async XLA Ops:
  52.7 5.0 %copy-start = (f32[2]{0:T(128)S(1)}, f32[2]{0:T(128)}, u32[]{:S(2)}) copy-start(f32[2]{0:T(128)} %get-tuple-element.19) | copy-start | bytes 28

commit v3 on v2

--- a/solution.py
+++ b/solution.py
@@ -196,23 +196,27 @@
 
     barrier = pltpu.get_barrier_semaphore()
 
-    @pl.loop(1, ny)
-    def _(k):
-        pl.semaphore_signal(barrier, inc=1, device_id=(x, lax.rem(y + k, ny)), device_id_type=MESH)
-
-    @pl.loop(1, nx)
-    def _(k):
-        pl.semaphore_signal(barrier, inc=1, device_id=(lax.rem(x + k, nx), y), device_id_type=MESH)
-
     expected = jnp.int32(nx - 1 + ny - 1)
     for dx, dy in MOVES:
+        there = inside(dx, dy)
         if dx and dy:
-            there = inside(dx, dy)
             expected = expected + there.astype(jnp.int32)
 
-            @pl.when(there)
-            def _():
-                pl.semaphore_signal(barrier, inc=1, device_id=(x + dx, y + dy), device_id_type=MESH)
+        @pl.when(there)
+        def _():
+            pl.semaphore_signal(barrier, inc=1, device_id=(x + dx, y + dy), device_id_type=MESH)
+
+    @pl.loop(0, nx)
+    def _(k):
+        @pl.when((k > x + 1) | (k < x - 1))
+        def _():
+            pl.semaphore_signal(barrier, inc=1, device_id=(k, y), device_id_type=MESH)
+
+    @pl.loop(0, ny)
+    def _(k):
+        @pl.when((k > y + 1) | (k < y - 1))
+        def _():
+            pl.semaphore_signal(barrier, inc=1, device_id=(x, k), device_id_type=MESH)
 
     loads = [
         pltpu.make_async_copy(src, dst, load_sem.at[i])
@@ -296,9 +300,6 @@
             result = result + total(value) * send_table[pl.ds(9 + i, 1)]
         return result
 
-    loads[0].wait()
-    loads[2].wait()
-    first_message = message(classes(lambda a: ext0[a + 1, own], weight_yz, (low_x, 1.0, high_x)))
     pl.semaphore_wait(barrier, expected)
 
     def copies(phase, source, target):
@@ -314,8 +315,8 @@
             for m, (dx, dy) in enumerate(MOVES)
         ]
 
-    def start(group):
-        for m in LONGEST_FIRST:
+    def start(group, moves=LONGEST_FIRST):
+        for m in moves:
             pl.when(inside(*MOVES[m]))(group[m].start)
 
     def arrive(group):
@@ -390,7 +391,7 @@
         half = matrix.shape[0] // 2
         return (out[half:, :128] + out[:half, 128:]) + out[:half, :128]
 
-    def solve(ext, loc):
+    def solve(ext, loc, group):
         h = (N + 2) // 2
         for i in range(h):
             lower, upper = ext[i], ext[N + 1 - i]
@@ -420,6 +421,8 @@
             out[pl.ds(N - 2, count, stride=N)] += from_above(out[pl.ds(count * N, count)])
 
         for i in range(h):
+            if i == 2:
+                start(group, LONGEST_FIRST[:6])
             for j in range(h):
                 at = pl.ds((i * h + j) * N, N)
                 ee, eo, oe, oo = oblk[0, at], oblk[1, at], oblk[2, at], oblk[3, at]
@@ -428,6 +431,7 @@
                 loc[N + 1 - i, one] = (ee + eo) - (oe + oo)
                 loc[i, two] = (ee - eo) + (oe - oo)
                 loc[N + 1 - i, two] = (ee - eo) - (oe - oo)
+        start(group, LONGEST_FIRST[6:])
 
     def spread_copies(phase, slot, loc):
         return copies(
@@ -443,26 +447,33 @@
 
     porosity = None
 
-    def apply(field, image):
+    def apply(field, image, group=None):
         for a in range(N // 2):
             lower, upper = field[a], field[N - 1 - a]
             ab[0, pl.ds(a * N * N, N * N)] = lower + upper
             ab[1, pl.ds(a * N * N, N * N)] = lower - upper
         even = product(stiff[0], ab[0])
         odd = product(stiff[1], ab[1])
-        for a in range(N // 2):
-            at = slice(a * N * N, (a + 1) * N * N)
-            scaled = mass[...] * F32(node_weights[a])
-            image[a] = porosity * (even[at] + odd[at]) + scaled * field[a]
-            image[N - 1 - a] = porosity * (even[at] - odd[at]) + scaled * field[N - 1 - a]
-        for a in range(N):
-            first = image[a, pl.ds(0, N, stride=N)]
-            final = image[a, pl.ds(N - 1, N, stride=N)]
-            image[a, pl.ds(0, N, stride=N)] = first + from_below(final)
-            image[a, pl.ds(N - 1, N, stride=N)] = final + from_above(first)
-
+        for i in range(N // 2):
+            at = slice(i * N * N, (i + 1) * N * N)
+            scaled = mass[...] * F32(node_weights[i])
+            image[i] = porosity * (even[at] + odd[at]) + scaled * field[i]
+            image[N - 1 - i] = porosity * (even[at] - odd[at]) + scaled * field[N - 1 - i]
+            for a in (i, N - 1 - i):
+                first = image[a, pl.ds(0, N, stride=N)]
+                final = image[a, pl.ds(N - 1, N, stride=N)]
+                image[a, pl.ds(0, N, stride=N)] = first + from_below(final)
+                image[a, pl.ds(N - 1, N, stride=N)] = final + from_above(first)
+            if i == 1 and group is not None:
+                start(group, LONGEST_FIRST[:6])
+        if group is not None:
+            start(group, LONGEST_FIRST[6:])
+
+    start(halo0)
+    loads[0].wait()
+    loads[2].wait()
+    first_message = total(weighted(lambda a: ext0[a + 1, own])) * send_table[pl.ds(4, 1)]
     gather_y(0, first_message)
-    start(halo0)
     for p in range(4):
         blk[p, pl.ds(248, 8)] = jnp.zeros((8, 128), F32)
     for i, load in enumerate(loads):
@@ -471,9 +482,8 @@
     porosity = 1.0 - 0.6 * grains[...].astype(F32) / MOST_GRAINS
     gather_x(0)
     arrive(halo0)
-    solve(ext0, loc0)
     spread0 = spread_copies(1, 0, loc0)
-    start(spread0)
+    solve(ext0, loc0, spread0)
     gathered(0)
     lifted(0)
     for a in range(N):
@@ -483,12 +493,6 @@
         area = node_area(d, dx, dy)
         area[...] += incoming(sides, corners, 0, m)[...]
 
-    apply(d, q1)
-    rho1 = weighted(lambda a: ext0[a + 1, own] * d[a])
-    curve = d[0] * q1[0]
-    for a in range(1, N):
-        curve = curve + d[a] * q1[a]
-    gather_y(1, message(classes(lambda a: q1[a], weight_z, (1.0, 1.0, 1.0)), rho1, weight_z * curve))
     faces = copies(
         2,
         lambda dx, dy: q1.at[
@@ -496,7 +500,12 @@
         ],
         lambda m: incoming(sides, corners, 1, m),
     )
-    start(faces)
+    apply(d, q1, faces)
+    rho1 = weighted(lambda a: ext0[a + 1, own] * d[a])
+    curve = d[0] * q1[0]
+    for a in range(1, N):
+        curve = curve + d[a] * q1[a]
+    gather_y(1, message(classes(lambda a: q1[a], weight_z, (1.0, 1.0, 1.0)), rho1, weight_z * curve))
     for i in (0, N + 1):
         ext1[i] = jnp.zeros_like(ext1[i])
     for a in range(N):
@@ -509,9 +518,8 @@
         area = ext1.at[span(*part(dx, (N, 2), (0, 2), (1, N))), span(*part(dy, (N, 2), (0, 2), (1, N)), N)]
         area[...] += incoming(sides, corners, 1, m)[...]
 
-    solve(ext1, loc1)
     spread1 = spread_copies(3, 2, loc1)
-    start(spread1)
+    solve(ext1, loc1, spread1)
     gathered(1)
     lifted(1)
     rho1, curve1 = sv[1, pl.ds(9, 1)], sv[1, pl.ds(10, 1)]
@@ -565,6 +573,19 @@
     steps_out[1] = step2[0, 0]
 
 
+def deliver(sol, res, direction, steps, sol_out, res_out, dir_out, steps_out, sems):
+    copies = [
+        pltpu.make_async_copy(src, dst, sems.at[i])
+        for i, (src, dst) in enumerate(
+            ((steps, steps_out), (sol, sol_out), (res, res_out), (direction, dir_out))
+        )
+    ]
+    for copy in copies:
+        copy.start()
+    for copy in copies:
+        copy.wait()
+
+
 def incoming(sides, corners, slot, m):
     first, second = MOVES[m]
     if first and second:
@@ -623,13 +644,24 @@
                 pltpu.SemaphoreType.DMA((3,)),
                 pltpu.SemaphoreType.DMA((3,)),
             ],
-            compiler_params=pltpu.CompilerParams(collective_id=0, has_side_effects=True),
+            compiler_params=pltpu.CompilerParams(collective_id=0, has_side_effects=True, vmem_limit_bytes=40 * 1024 * 1024),
             name="cg_steps",
         )(
+            *(pltpu.with_memory_space_constraint(v, pltpu.HBM) for v in (
             sol.reshape(flat), res.reshape(flat), grains,
             jnp.asarray(schwarz), jnp.asarray(stiff), jnp.asarray(send), jnp.asarray(along_x),
-            jnp.asarray(back), jnp.asarray(mass),
+            jnp.asarray(back), jnp.asarray(mass),))
         )
+        hbm = pl.BlockSpec(memory_space=pltpu.HBM)
+        outs = pl.pallas_call(
+            deliver,
+            out_shape=(out, out, out, jax.ShapeDtypeStruct((2,), F32)),
+            in_specs=[anywhere] * 4,
+            out_specs=(hbm,) * 4,
+            scratch_shapes=[pltpu.SemaphoreType.DMA((4,))],
+            compiler_params=pltpu.CompilerParams(vmem_limit_bytes=2 * 1024 * 1024),
+            name="deliver",
+        )(*outs)
         return tuple(v.reshape(shape) for v in outs[:3]) + (outs[3],)
 
     wide_spec = P("gx", "gy", None, None, None, None)

time: 58.5 us -> 53.7 us (0.918)
  local copies, waits for them, and re-layouts: 5.53 us -> 0 us
  Pallas kernels: 52.1 us -> 52.9 us
    unnamed x6 -> x0, local copies, waits for them, and re-layouts: 5.53 us -> none
    pallas_call x0 -> x1, Pallas kernels: none -> 0.92 us  [step(): pl.pallas_call(deliver, out_shape=(out, out, out, jax.ShapeDtypeStruct((2...]
where the time goes in v3:
time: 53.7 us; the launch traced here: 53.6 us
  Pallas kernels  52.9 us (99%)
  between operations  0.64 us (1%)
    pallas_call x1, Pallas kernels, step(): pl.pallas_call(functools.partial(kernel, nx, ny, [float(v) for v in weigh...  52 us

profile of v3, /device:TPU:1, one launch (start us, length us, event | category | flops | bytes accessed | tf_op | source)
XLA Modules:
  0.0 53.6 jit_solution(12592545423260248393)
XLA Ops:
  0.6 52.0 %cg_steps.1 = (f32[1,1,8,64,128]{4,3,2,1,0:T(8,128)S(1)}, f32[1,1,8,64,128]{4,3,2,1,0:T(8,128)S(1)}, f32[1,1,8,64,128]{4,3,2,1,0:T(8,128)S(1)}, f32[2]{0:T(128)S(1)}) custom-call(f32[1,1,8,64,128]{4,3,2,1,0:T(8,128)} %bitcast.5, f32[1,1,8,64,128]{4,3,2,1,0:T(8,128)} %bitcast.6, s32[1,1,128]{2,1,0:T(1,128)} %grains_in.1, ...), custom_call_target="tpu_custom_call" | custom-call | tf_op jit(solution)/shard_map/cg_steps/pallas_call | solution.py:613
  52.6 0.9 %deliver.1 = (f32[1,1,8,64,128]{4,3,2,1,0:T(8,128)}, f32[1,1,8,64,128]{4,3,2,1,0:T(8,128)}, f32[1,1,8,64,128]{4,3,2,1,0:T(8,128)}, f32[2]{0:T(128)}) custom-call(f32[1,1,8,64,128]{4,3,2,1,0:T(8,128)S(1)} %get-tuple-element.12.sol, f32[1,1,8,64,128]{4,3,2,1,0:T(8,128)S(1)} %get-tuple-element.13.res, f32[1,1,8,64,128]{4,3,2,1,0:T(8,128)S(1)} %get-tuple-element.14.direction, ...), custom_call_target="tpu_custom_call" | custom-call | tf_op jit(solution)/shard_map/deliver/pallas_call | solution.py:656

commit v4 on v3

--- a/solution.py
+++ b/solution.py
@@ -19,6 +19,7 @@
 BF16 = jnp.bfloat16
 MOVES = [(1, 0), (-1, 0), (0, 1), (0, -1), (1, 1), (1, -1), (-1, 1), (-1, -1)]
 LONGEST_FIRST = [4, 5, 6, 7, 0, 1, 2, 3]
+NEAREST_FIRST = [2, 3, 0, 1, 4, 5, 6, 7]
 PLAIN = 48
 
 
@@ -68,7 +69,7 @@
 def hi_lo(matrix):
     high = matrix.astype(ml_dtypes.bfloat16)
     low = (matrix - high.astype(np.float64)).astype(ml_dtypes.bfloat16)
-    return np.concatenate([high, low], axis=-2)
+    return np.concatenate([high, low], axis=-1)
 
 
 def schwarz_blocks():
@@ -223,12 +224,14 @@
         for i, (src, dst) in enumerate(
             [
                 (res_in.at[0, 0], ext0.at[pl.ds(1, N), pl.ds(N, N * N)]),
-                (schwarz_in, schwarz),
+                (schwarz_in, schwarz.at[:, :, pl.ds(0, 512)]),
                 (send_in.at[y], send_table),
                 (along_x_in.at[x], along_x),
                 (back_in.at[y], back),
                 (grains_in.at[0], grains),
-                (stiff_in, stiff),
+                (stiff_in, stiff.at[:, :, pl.ds(0, 512)]),
+                (schwarz_in.at[:, :, pl.ds(0, 256)], schwarz.at[:, :, pl.ds(512, 256)]),
+                (stiff_in.at[:, :, pl.ds(0, 256)], stiff.at[:, :, pl.ds(512, 256)]),
                 (mass_in, mass),
                 (sol_in.at[0, 0], sol),
             ]
@@ -241,10 +244,6 @@
 
         @pl.when(jnp.logical_not(inside(-dx, -dy)))
         def _():
-            for phase in range(3):
-                incoming(sides, corners, phase, m)[...] = jnp.zeros_like(incoming(sides, corners, phase, m))
-            edge = incoming(sides1, corners1, None, m)
-            edge[...] = jnp.zeros_like(edge)
             area = ext0.at[span(*part(dx, (N + 1, 1), (0, 1), (1, N))), span(*part(dy, (N + 1, 1), (0, 1), (1, N)), N)]
             area[...] = jnp.zeros_like(area)
 
@@ -300,6 +299,9 @@
             result = result + total(value) * send_table[pl.ds(9 + i, 1)]
         return result
 
+    loads[0].wait()
+    loads[2].wait()
+    first_message = total(weighted(lambda a: ext0[a + 1, own])) * send_table[pl.ds(4, 1)]
     pl.semaphore_wait(barrier, expected)
 
     def copies(phase, source, target):
@@ -323,6 +325,17 @@
         for m, (dx, dy) in enumerate(MOVES):
             pl.when(inside(-dx, -dy))(group[m].wait_recv)
 
+    def arrive_and_add(group, area, slot, scale=None):
+        for m in NEAREST_FIRST:
+            dx, dy = MOVES[m]
+
+            @pl.when(inside(-dx, -dy))
+            def _():
+                group[m].wait_recv()
+                target = area(dx, dy)
+                value = incoming(*slot, m)[...]
+                target[...] += value if scale is None else scale * value
+
     def sent(group):
         for m, (dx, dy) in enumerate(MOVES):
             pl.when(inside(dx, dy))(group[m].wait_send)
@@ -365,7 +378,7 @@
 
     def gather_x(g):
         all_rows(buf_y.at[g], gy_send.at[g], gy_recv.at[g], ny)
-        value = jnp.sum(buf_y[g].reshape(ny, 128), axis=0, keepdims=True)
+        value = jnp.sum(buf_y[g], axis=0)
         buf_x[g, pl.ds(x, 1)] = value.reshape(1, 1, 128)
         stage(buf_x.at[g], x, gx_send.at[g], gx_recv.at[g], nx, lambda k: (lax.rem(x + k, nx), y))
 
@@ -387,9 +400,7 @@
     def product(matrix, v):
         high = v.astype(BF16)
         low = (v - high.astype(F32)).astype(BF16)
-        out = jnp.dot(matrix, jnp.concatenate([high, low], axis=1), preferred_element_type=F32)
-        half = matrix.shape[0] // 2
-        return (out[half:, :128] + out[:half, 128:]) + out[:half, :128]
+        return jnp.dot(matrix, jnp.concatenate([high, high, low], axis=0), preferred_element_type=F32)
 
     def solve(ext, loc, group):
         h = (N + 2) // 2
@@ -405,14 +416,15 @@
                 blk[3, at] = odd[one] - odd[two]
         count = h * h
 
-        @pl.loop(0, 4)
-        def _(p):
-            source, out = blk.at[p], oblk.at[p]
+        for p in range(4):
+            source = blk.at[p]
             below = source[pl.ds(N - 2, count, stride=N)]
             above = source[pl.ds(1, count, stride=N)]
             source[pl.ds(count * N, count)] = from_below(below)
             source[pl.ds(count * (N + 1), count)] = from_above(above)
-            out[...] = product(schwarz[p], source[...])
+        for p in range(4):
+            out = oblk.at[p]
+            out[...] = product(schwarz[p], blk[p])
             first = out[pl.ds(0, count, stride=N)]
             final = out[pl.ds(N - 1, count, stride=N)]
             out[pl.ds(0, count, stride=N)] = first + from_below(final)
@@ -469,11 +481,8 @@
         if group is not None:
             start(group, LONGEST_FIRST[6:])
 
+    gather_y(0, first_message)
     start(halo0)
-    loads[0].wait()
-    loads[2].wait()
-    first_message = total(weighted(lambda a: ext0[a + 1, own])) * send_table[pl.ds(4, 1)]
-    gather_y(0, first_message)
     for p in range(4):
         blk[p, pl.ds(248, 8)] = jnp.zeros((8, 128), F32)
     for i, load in enumerate(loads):
@@ -488,10 +497,7 @@
     lifted(0)
     for a in range(N):
         d[a] = loc0[a + 1, own] + lift[0 if a == 0 else (2 if a == N - 1 else 1)]
-    arrive(spread0)
-    for m, (dx, dy) in enumerate(MOVES):
-        area = node_area(d, dx, dy)
-        area[...] += incoming(sides, corners, 0, m)[...]
+    arrive_and_add(spread0, lambda dx, dy: node_area(d, dx, dy), (sides, corners, 0))
 
     faces = copies(
         2,
@@ -513,10 +519,11 @@
         ext1[a + 1, own] = q1[a]
         ext1[a + 1, pl.ds(N * N + N, N)] = jnp.zeros((N, 128), F32)
     gather_x(1)
-    arrive(faces)
-    for m, (dx, dy) in enumerate(MOVES):
-        area = ext1.at[span(*part(dx, (N, 2), (0, 2), (1, N))), span(*part(dy, (N, 2), (0, 2), (1, N)), N)]
-        area[...] += incoming(sides, corners, 1, m)[...]
+    arrive_and_add(
+        faces,
+        lambda dx, dy: ext1.at[span(*part(dx, (N, 2), (0, 2), (1, N))), span(*part(dy, (N, 2), (0, 2), (1, N)), N)],
+        (sides, corners, 1),
+    )
 
     spread1 = spread_copies(3, 2, loc1)
     solve(ext1, loc1, spread1)
@@ -528,10 +535,7 @@
         z2[a] = d[a] - step1 * (loc1[a + 1, own] + lift[0 if a == 0 else (2 if a == N - 1 else 1)])
         r1[a] = ext0[a + 1, own] - step1 * ext1[a + 1, own]
         sol[a] = sol[a] + step1 * d[a]
-    arrive(spread1)
-    for m, (dx, dy) in enumerate(MOVES):
-        area = node_area(z2, dx, dy)
-        area[...] -= step1 * incoming(sides, corners, 2, m)[...]
+    arrive_and_add(spread1, lambda dx, dy: node_area(z2, dx, dy), (sides, corners, 2), -step1)
 
     apply(z2, q2)
     curve_new = z2[0] * q2[0]
@@ -552,16 +556,20 @@
     for a in range(N):
         im2[a] = q2[a]
     gather_x(2)
-    arrive(edges)
-    for m, (dx, dy) in enumerate(MOVES):
-        area = im2.at[
+    arrive_and_add(
+        edges,
+        lambda dx, dy: im2.at[
             span(*part(dx, (N - 1, 1), (0, 1), (0, N))), span(*part(dy, (N - 1, 1), (0, 1), (0, N)), N)
-        ]
-        area[...] += incoming(sides1, corners1, None, m)[...]
+        ],
+        (sides1, corners1, None),
+    )
     for group in (halo0, spread0, faces, spread1, edges):
         sent(group)
-    gathered(2)
-    rho2, curve_new, curve_mixed = sv[2, pl.ds(9, 1)], sv[2, pl.ds(10, 1)], sv[2, pl.ds(11, 1)]
+    all_rows(buf_x.at[2], gx_send.at[2], gx_recv.at[2], nx)
+    value = jnp.sum(buf_x[2], axis=0)
+    rho2, curve_new, curve_mixed = (
+        jnp.sum(jnp.where(lane == PLAIN + 16 * i, value, 0.0), axis=1, keepdims=True) for i in range(3)
+    )
     ratio = rho2 / rho1
     step2 = rho2 / (curve_new + ratio * (2.0 * curve_mixed + ratio * curve1))
     for a in range(N):
@@ -618,8 +626,8 @@
             scratch_shapes=[
                 field, wide, wide,
                 pltpu.VMEM((1, 128), jnp.int32),
-                pltpu.VMEM((4, 512, 256), BF16),
-                pltpu.VMEM((2, 512, 256), BF16),
+                pltpu.VMEM((4, 256, 768), BF16),
+                pltpu.VMEM((2, 256, 768), BF16),
                 pltpu.VMEM((16, 128), F32),
                 pltpu.VMEM((3, nx, 128), F32),
                 pltpu.VMEM((16, 128), F32),
@@ -636,7 +644,7 @@
                 pltpu.VMEM((3, 4, 2, 2 * N, 128), F32),
                 [pltpu.VMEM((2, 1, nn, 128), F32), pltpu.VMEM((2, N, N, 128), F32)],
                 pltpu.VMEM((4, 1, N, 128), F32),
-                pltpu.SemaphoreType.DMA((9,)),
+                pltpu.SemaphoreType.DMA((11,)),
                 pltpu.SemaphoreType.DMA((5, 8)),
                 pltpu.SemaphoreType.DMA((5, 8)),
                 pltpu.SemaphoreType.DMA((3,)),

time: 53.7 us -> 52 us (0.968)
  Pallas kernels: 52.9 us -> 51.2 us
    pallas_call x1, Pallas kernels: 52 us -> 50.3 us  [step(): pl.pallas_call(functools.partial(kernel, nx, ny, [float(v) for v in weigh...]
where the time goes in v4:
time: 52 us; the launch traced here: 51.8 us
  Pallas kernels  51.2 us (98%)
  between operations  0.64 us (1%)
    pallas_call x1, Pallas kernels, step(): pl.pallas_call(functools.partial(kernel, nx, ny, [float(v) for v in weigh...  50.3 us

profile of v4, /device:TPU:1, one launch (start us, length us, event | category | flops | bytes accessed | tf_op | source)
XLA Modules:
  0.0 51.8 jit_solution(15081336410860225484)
XLA Ops:
  0.6 50.3 %cg_steps.1 = (f32[1,1,8,64,128]{4,3,2,1,0:T(8,128)S(1)}, f32[1,1,8,64,128]{4,3,2,1,0:T(8,128)S(1)}, f32[1,1,8,64,128]{4,3,2,1,0:T(8,128)S(1)}, f32[2]{0:T(128)S(1)}) custom-call(f32[1,1,8,64,128]{4,3,2,1,0:T(8,128)} %bitcast.5, f32[1,1,8,64,128]{4,3,2,1,0:T(8,128)} %bitcast.6, s32[1,1,128]{2,1,0:T(1,128)} %grains_in.1, ...), custom_call_target="tpu_custom_call" | custom-call | tf_op jit(solution)/shard_map/cg_steps/pallas_call | solution.py:621
  50.9 0.9 %deliver.1 = (f32[1,1,8,64,128]{4,3,2,1,0:T(8,128)}, f32[1,1,8,64,128]{4,3,2,1,0:T(8,128)}, f32[1,1,8,64,128]{4,3,2,1,0:T(8,128)}, f32[2]{0:T(128)}) custom-call(f32[1,1,8,64,128]{4,3,2,1,0:T(8,128)S(1)} %get-tuple-element.12.sol, f32[1,1,8,64,128]{4,3,2,1,0:T(8,128)S(1)} %get-tuple-element.13.res, f32[1,1,8,64,128]{4,3,2,1,0:T(8,128)S(1)} %get-tuple-element.14.direction, ...), custom_call_target="tpu_custom_call" | custom-call | tf_op jit(solution)/shard_map/deliver/pallas_call | solution.py:664

commit v5 on v4

--- a/solution.py
+++ b/solution.py
@@ -537,14 +537,16 @@
         sol[a] = sol[a] + step1 * d[a]
     arrive_and_add(spread1, lambda dx, dy: node_area(z2, dx, dy), (sides, corners, 2), -step1)
 
+    rho2 = jnp.sum(weighted(lambda a: r1[a] * z2[a]), axis=0, keepdims=True)
+    curve_mixed = z2[0] * q1[0]
+    for a in range(1, N):
+        curve_mixed = curve_mixed + z2[a] * q1[a]
+    curve_mixed = jnp.sum(weight_z * curve_mixed, axis=0, keepdims=True)
     apply(z2, q2)
     curve_new = z2[0] * q2[0]
-    curve_mixed = z2[0] * q1[0]
     for a in range(1, N):
         curve_new = curve_new + z2[a] * q2[a]
-        curve_mixed = curve_mixed + z2[a] * q1[a]
-    rho2 = weighted(lambda a: r1[a] * z2[a])
-    gather_y(2, message([], rho2, weight_z * curve_new, weight_z * curve_mixed))
+    gather_y(2, message([], rho2, weight_z * curve_new, curve_mixed))
     edges = copies(
         4,
         lambda dx, dy: q2.at[

time: 52 us -> 52 us (level)
  no operation moved by 1% of the time
where the time goes in v5:
time: 52 us; the launch traced here: 51.8 us
  Pallas kernels  51.2 us (98%)
  between operations  0.64 us (1%)
    pallas_call x1, Pallas kernels, step(): pl.pallas_call(functools.partial(kernel, nx, ny, [float(v) for v in weigh...  50.3 us

profile of v5, /device:TPU:1, one launch (start us, length us, event | category | flops | bytes accessed | tf_op | source)
XLA Modules:
  0.0 51.8 jit_solution(5342226064323470762)
XLA Ops:
  0.6 50.3 %cg_steps.1 = (f32[1,1,8,64,128]{4,3,2,1,0:T(8,128)S(1)}, f32[1,1,8,64,128]{4,3,2,1,0:T(8,128)S(1)}, f32[1,1,8,64,128]{4,3,2,1,0:T(8,128)S(1)}, f32[2]{0:T(128)S(1)}) custom-call(f32[1,1,8,64,128]{4,3,2,1,0:T(8,128)} %bitcast.5, f32[1,1,8,64,128]{4,3,2,1,0:T(8,128)} %bitcast.6, s32[1,1,128]{2,1,0:T(1,128)} %grains_in.1, ...), custom_call_target="tpu_custom_call" | custom-call | tf_op jit(solution)/shard_map/cg_steps/pallas_call | solution.py:623
  50.9 0.9 %deliver.1 = (f32[1,1,8,64,128]{4,3,2,1,0:T(8,128)}, f32[1,1,8,64,128]{4,3,2,1,0:T(8,128)}, f32[1,1,8,64,128]{4,3,2,1,0:T(8,128)}, f32[2]{0:T(128)}) custom-call(f32[1,1,8,64,128]{4,3,2,1,0:T(8,128)S(1)} %get-tuple-element.12.sol, f32[1,1,8,64,128]{4,3,2,1,0:T(8,128)S(1)} %get-tuple-element.13.res, f32[1,1,8,64,128]{4,3,2,1,0:T(8,128)S(1)} %get-tuple-element.14.direction, ...), custom_call_target="tpu_custom_call" | custom-call | tf_op jit(solution)/shard_map/deliver/pallas_call | solution.py:666
